TPU v7x, 512 devices: a whole 4x8x8 slice. The times are simulated.
512 devices in a mesh: ta: 8 (over y_lo, core), gx: 8 (over y_hi, x), gy: 8 (over z).
Axes of the slice: x: 4, y: 8 (y_hi: 2, y_lo: 4; y = y_hi * 4 + y_lo), z: 8, core: 2. Of those that a mesh axis runs over, the one named last changes fastest.
Arguments:
- density: float32 [64, 512, 1024], P('ta', 'gx', 'gy'), may hold values from 0.25 to 9.5
- flux_x: float32 [64, 512, 1024], P('ta', 'gx', 'gy'), may hold values from -14 to 14
- flux_y: float32 [64, 512, 1024], P('ta', 'gx', 'gy'), may hold values from -14 to 14
- congestion: float32 [64, 512, 1024], P('ta', 'gx', 'gy'), may hold values from 0.2 to 5
- initial_density: float32 [512, 1024], P('gx', 'gy'), may hold values from 0.25 to 2.5
Outputs:
- mass_out: float32 [64, 512, 1024], P('ta', 'gx', 'gy')
- flux_x_out: float32 [64, 512, 1024], P('ta', 'gx', 'gy')
- flux_y_out: float32 [64, 512, 1024], P('ta', 'gx', 'gy')
All inputs are finite; a program needn't handle non-finite values.
Results may differ from a plain program's by a relative error of at most 0.0003.
Values sent between devices are 32-bit elements; how exact they have to be, the bound alone decides.
A program may use at most 64 MiB of HBM per device.

v0:
```python
import jax
import jax.numpy as jnp
from jax import lax
from jax.sharding import PartitionSpec as P

ITERS = 3
NEWTON = 6


step_gamma = 1.0


def padded_2(cells, sides, width):
    for axis, dim in sides:
        count = lax.axis_size(axis)
        head = lax.slice_in_dim(cells, 0, width, axis=dim)
        tail = lax.slice_in_dim(cells, cells.shape[dim] - width, cells.shape[dim], axis=dim)
        cells = jnp.concatenate(
            [
                lax.ppermute(tail, axis, [(i, (i + 1) % count) for i in range(count)]),
                cells,
                lax.ppermute(head, axis, [((i + 1) % count, i) for i in range(count)]),
            ],
            axis=dim,
        )
    return cells


def neighbour_faces(grid_vals, lower_end, upper_end):
    padded = padded_2(grid_vals, (("ta", 0), ("gx", 1), ("gy", 2)), 1)
    lower_rim = padded[0, 1:-1, 1:-1]
    upper_rim = padded[-1, 1:-1, 1:-1]
    x_planes = padded[1:-1, :, 1:-1]
    y_planes = padded[1:-1, 1:-1, :]
    is_first = lax.axis_index("ta") == 0
    is_last = lax.axis_index("ta") == lax.axis_size("ta") - 1
    lower_rim = jnp.where(is_first, lower_end, lower_rim)
    upper_rim = jnp.where(is_last, upper_end, upper_rim)
    earlier = jnp.concatenate([lower_rim[None], grid_vals[:-1]], 0)
    later = jnp.concatenate([grid_vals[1:], upper_rim[None]], 0)
    return (
        earlier,
        later,
        x_planes[:, :-2],
        x_planes[:, 2:],
        y_planes[:, :, :-2],
        y_planes[:, :, 2:],
    )


def laplacian(potential):
    zero_plane = jnp.zeros_like(potential[0])
    earlier, later, x_before, x_after, y_before, y_after = neighbour_faces(
        potential, potential[0], zero_plane
    )
    result = 6.0 * potential - earlier - later
    result = result - x_before - x_after
    return result - y_before - y_after


def squares(residual):
    return lax.psum(jnp.sum(residual * residual), ("ta", "gx", "gy"))


def body(density, flux_x, flux_y, congestion, initial_density):
    speed_sq = flux_x * flux_x + flux_y * flux_y
    slope_coef = 1.0 + step_gamma * congestion
    mass_new = jnp.zeros_like(density)
    for newton in range(NEWTON):
        shifted = mass_new + step_gamma
        mismatch = (
            slope_coef * mass_new - density - step_gamma * speed_sq / (2.0 * shifted * shifted)
        )
        derivative = slope_coef + step_gamma * speed_sq / (shifted * shifted * shifted)
        mass_new = mass_new - mismatch / derivative
    shrink = mass_new / (mass_new + step_gamma)
    prox_x = flux_x * shrink
    prox_y = flux_y * shrink
    zero_plane = jnp.zeros_like(density[0])
    mass_before = neighbour_faces(mass_new, initial_density, zero_plane)[0]
    x_before = neighbour_faces(prox_x, zero_plane, zero_plane)[2]
    y_before = neighbour_faces(prox_y, zero_plane, zero_plane)[4]
    source = mass_new - mass_before + prox_x - x_before + prox_y - y_before
    potential = jnp.zeros_like(source)
    residual = source
    direction = source
    norm_now = squares(residual)
    for iteration in range(ITERS):
        applied = laplacian(direction)
        step_size = norm_now / lax.psum(jnp.sum(direction * applied), ("ta", "gx", "gy"))
        potential = potential + step_size * direction
        residual = residual - step_size * applied
        norm_next = squares(residual)
        direction = residual + norm_next / norm_now * direction
        norm_now = norm_next
    earlier, later, x_before, x_after, y_before, y_after = neighbour_faces(
        potential, potential[0], zero_plane
    )
    mass_out = mass_new - (potential - later)
    flux_x_out = prox_x - (potential - x_after)
    flux_y_out = prox_y - (potential - y_after)
    return (mass_out, flux_x_out, flux_y_out)


def solution(mesh):
    placed = (
        P("ta", "gx", "gy"),
        P("ta", "gx", "gy"),
        P("ta", "gx", "gy"),
        P("ta", "gx", "gy"),
        P("gx", "gy"),
    )
    return jax.shard_map(
        body,
        mesh=mesh,
        in_specs=placed,
        out_specs=(P("ta", "gx", "gy"), P("ta", "gx", "gy"), P("ta", "gx", "gy")),
        check_vma=False,
    )
```

profile of v0, /device:TPU:1, one launch (start us, length us, event | category | flops | bytes accessed | tf_op | source)
XLA Modules:
  0.0 702.6 jit_solution(4112889658601952940)
XLA Ops:
  0.6 2.2 fusion.57
  2.8 4.6 collective-permute-start
  7.5 1.9 collective-permute-start.4
  9.4 6.1 collective-permute-start.5
  15.6 1.9 collective-permute-start.1
  17.5 5.4 collective-permute-start.2
  23.0 1.9 collective-permute-start.6
  24.9 9.4 %collective-permute-start.7 = (f32[10,1,128]{2,1,0:T(1,128)S(1)}, f32[10,1,128]{2,1,0:T(1,128)S(1)}, u32[]{:S(2)}, u32[]{:S(2)}) collective-permute-start(f32[10,1,128]{2,1,0:T(1,128)S(1)} %get-tuple-element.31), channel_id=1, source_target_pairs={{8,0},{16,8},{24,16},{32,24},{40,32},{48,40},{56,48},{0,56},{9,1},... | collective-permute-start | bytes 15368 | tf_op jit(solution)/shard_map/ppermute | solution.py:22
  34.4 1.9 collective-permute-start.3
  36.5 1.9 collective-permute-start.8
  38.5 6.3 collective-permute-done.3
  44.8 2.5 collective-permute-done.8
  47.4 6.5 collective-permute-start.9
  54.0 1.0 collective-permute-done.9
  55.0 5.8 collective-permute-start.10
  61.6 1.9 collective-permute-start.11
  63.6 9.7 %collective-permute-start.12 = (f32[10,1,128]{2,1,0:T(1,128)S(1)}, f32[10,1,128]{2,1,0:T(1,128)S(1)}, u32[]{:S(2)}, u32[]{:S(2)}) collective-permute-start(f32[10,1,128]{2,1,0:T(1,128)S(1)} %get-tuple-element.29), channel_id=1, source_target_pairs={{8,0},{16,8},{24,16},{32,24},{40,32},{48,40},{56,48},{0,56},{9,1},... | collective-permute-start | bytes 15368 | tf_op jit(solution)/shard_map/ppermute | solution.py:22
  74.2 1.9 collective-permute-start.13
  76.1 4.6 collective-permute-start.14
  80.7 5.1 collective-permute-done.13
  87.6 105.8 %all-reduce = (f32[]{:T(128)}, f32[]{:T(128)}) all-reduce(f32[]{:T(128)} %get-tuple-element.4, f32[]{:T(128)} %get-tuple-element.3), channel_id=1, replica_groups=mesh['ta'=8,'gx'=8,'gy'=8] {'ta','gx','gy'}, use_global_device_ids=true, to_apply=%region_1.2 | all-reduce | flops 2 | bytes 16 | tf_op jit(solution)/shard_map/psum | solution.py:62
  195.4 94.8 %psum.44 = f32[]{:T(128)} all-reduce(f32[]{:T(128)} %get-tuple-element.9), channel_id=1, replica_groups=mesh['ta'=8,'gx'=8,'gy'=8] {'ta','gx','gy'}, use_global_device_ids=true, to_apply=%region_5.6 | all-reduce | flops 1 | bytes 8 | tf_op jit(solution)/shard_map/psum | solution.py:62
  291.6 3.2 collective-permute-start.15
  294.8 1.0 collective-permute-done.15
  295.8 5.3 collective-permute-start.16
  302.0 3.7 collective-permute-start.17
  305.7 7.6 %collective-permute-start.18 = (f32[10,1,128]{2,1,0:T(1,128)S(1)}, f32[10,1,128]{2,1,0:T(1,128)S(1)}, u32[]{:S(2)}, u32[]{:S(2)}) collective-permute-start(f32[10,1,128]{2,1,0:T(1,128)S(1)} %get-tuple-element.27), channel_id=1, source_target_pairs={{8,0},{16,8},{24,16},{32,24},{40,32},{48,40},{56,48},{0,56},{9,1},... | collective-permute-start | bytes 15368 | tf_op jit(solution)/shard_map/ppermute | solution.py:22
  314.3 1.9 collective-permute-start.19
  316.2 4.6 collective-permute-start.20
  320.8 4.8 collective-permute-done.19
  327.4 105.8 %psum.45 = f32[]{:T(128)} all-reduce(f32[]{:T(128)} %get-tuple-element.7), channel_id=1, replica_groups=mesh['ta'=8,'gx'=8,'gy'=8] {'ta','gx','gy'}, use_global_device_ids=true, to_apply=%region_7.8 | all-reduce | flops 1 | bytes 8 | tf_op jit(solution)/shard_map/psum | solution.py:90
  435.2 93.2 %psum.46 = f32[]{:T(128)} all-reduce(f32[]{:T(128)} %multiply_reduce_fusion), channel_id=1, replica_groups=mesh['ta'=8,'gx'=8,'gy'=8] {'ta','gx','gy'}, use_global_device_ids=true, to_apply=%region_9.10 | all-reduce | flops 1 | bytes 8 | tf_op jit(solution)/shard_map/psum | solution.py:62
  529.8 2.9 collective-permute-start.21
  533.7 5.7 collective-permute-start.22
  540.2 3.7 collective-permute-start.23
  543.9 7.6 %collective-permute-start.24 = (f32[10,1,128]{2,1,0:T(1,128)S(1)}, f32[10,1,128]{2,1,0:T(1,128)S(1)}, u32[]{:S(2)}, u32[]{:S(2)}) collective-permute-start(f32[10,1,128]{2,1,0:T(1,128)S(1)} %get-tuple-element.25), channel_id=1, source_target_pairs={{8,0},{16,8},{24,16},{32,24},{40,32},{48,40},{56,48},{0,56},{9,1},... | collective-permute-start | bytes 15368 | tf_op jit(solution)/shard_map/ppermute | solution.py:22
  552.5 2.4 collective-permute-start.25
  554.9 4.1 collective-permute-start.26
  559.0 4.8 collective-permute-done.25
  565.6 105.0 %psum.47 = f32[]{:T(128)} all-reduce(f32[]{:T(128)} %fusion.36), channel_id=1, replica_groups=mesh['ta'=8,'gx'=8,'gy'=8] {'ta','gx','gy'}, use_global_device_ids=true, to_apply=%region_11.12 | all-reduce | flops 1 | bytes 8 | tf_op jit(solution)/shard_map/psum | solution.py:90
  672.0 1.9 collective-permute-start.28
  673.9 2.6 collective-permute-start.27
  676.6 2.8 collective-permute-done.27
  679.5 1.9 collective-permute-start.30
  681.4 9.4 %collective-permute-start.29 = (f32[10,1,128]{2,1,0:T(1,128)S(1)}, f32[10,1,128]{2,1,0:T(1,128)S(1)}, u32[]{:S(2)}, u32[]{:S(2)}) collective-permute-start(f32[10,1,128]{2,1,0:T(1,128)S(1)} %get-tuple-element.23), channel_id=1, source_target_pairs={{8,0},{16,8},{24,16},{32,24},{40,32},{48,40},{56,48},{0,56},{9,1},... | collective-permute-start | bytes 15368 | tf_op jit(solution)/shard_map/ppermute | solution.py:22
  691.6 3.7 collective-permute-start.31
  695.3 6.3 collective-permute-done.31
  701.6 1.0 fusion.31
  (71 shorter events, 14.6 us)
Async XLA Ops:
  0.6 6.8 copy-start
  2.8 35.6 %collective-permute-start = (f32[1,64,128]{2,1,0:T(8,128)S(1)}, f32[1,64,128]{2,1,0:T(8,128)S(1)}, u32[]{:S(2)}, u32[]{:S(2)}) collective-permute-start(f32[1,64,128]{2,1,0:T(8,128)S(1)} %slice.279), channel_id=1, source_target_pairs={{0,64},{64,128},{128,192},{192,256},{256,320},{320,384},{384,448},... | collective-permute-start | bytes 98312 | tf_op jit(solution)/shard_map/ppermute | solution.py:20
  7.5 15.5 %collective-permute-start.4 = (f32[1,64,128]{2,1,0:T(8,128)S(1)}, f32[1,64,128]{2,1,0:T(8,128)S(1)}, u32[]{:S(2)}, u32[]{:S(2)}) collective-permute-start(f32[1,64,128]{2,1,0:T(8,128)S(1)} %get-tuple-element.49), channel_id=1, source_target_pairs={{0,64},{64,128},{128,192},{192,256},{256,320},{320,384},{384,448},... | collective-permute-start | bytes 98312 | tf_op jit(solution)/shard_map/ppermute | solution.py:20
  9.4 13.6 %collective-permute-start.5 = (f32[1,64,128]{2,1,0:T(8,128)S(1)}, f32[1,64,128]{2,1,0:T(8,128)S(1)}, u32[]{:S(2)}, u32[]{:S(2)}) collective-permute-start(f32[1,64,128]{2,1,0:T(8,128)S(1)} %get-tuple-element.50), channel_id=1, source_target_pairs={{64,0},{128,64},{192,128},{256,192},{320,256},{384,320},{448,384},... | collective-permute-start | bytes 98312 | tf_op jit(solution)/shard_map/ppermute | solution.py:22
  15.6 18.8 %collective-permute-start.1 = (f32[1,64,128]{2,1,0:T(8,128)S(1)}, f32[1,64,128]{2,1,0:T(8,128)S(1)}, u32[]{:S(2)}, u32[]{:S(2)}) collective-permute-start(f32[1,64,128]{2,1,0:T(8,128)S(1)} %get-tuple-element.47), channel_id=1, source_target_pairs={{0,64},{64,128},{128,192},{192,256},{256,320},{320,384},{384,448},... | collective-permute-start | bytes 98312 | tf_op jit(solution)/shard_map/ppermute | solution.py:20
  17.5 16.9 %collective-permute-start.2 = (f32[1,64,128]{2,1,0:T(8,128)S(1)}, f32[1,64,128]{2,1,0:T(8,128)S(1)}, u32[]{:S(2)}, u32[]{:S(2)}) collective-permute-start(f32[1,64,128]{2,1,0:T(8,128)S(1)} %get-tuple-element.48), channel_id=1, source_target_pairs={{64,0},{128,64},{192,128},{256,192},{320,256},{384,320},{448,384},... | collective-permute-start | bytes 98312 | tf_op jit(solution)/shard_map/ppermute | solution.py:22
  23.0 13.3 %collective-permute-start.6 = (f32[10,1,128]{2,1,0:T(1,128)S(1)}, f32[10,1,128]{2,1,0:T(1,128)S(1)}, u32[]{:S(2)}, u32[]{:S(2)}) collective-permute-start(f32[10,1,128]{2,1,0:T(1,128)S(1)} %get-tuple-element.30), channel_id=1, source_target_pairs={{0,8},{8,16},{16,24},{24,32},{32,40},{40,48},{48,56},{56,0},{1,9},... | collective-permute-start | bytes 15368 | tf_op jit(solution)/shard_map/ppermute | solution.py:20
  24.9 11.4 %collective-permute-start.7 = (f32[10,1,128]{2,1,0:T(1,128)S(1)}, f32[10,1,128]{2,1,0:T(1,128)S(1)}, u32[]{:S(2)}, u32[]{:S(2)}) collective-permute-start(f32[10,1,128]{2,1,0:T(1,128)S(1)} %get-tuple-element.31), channel_id=1, source_target_pairs={{8,0},{16,8},{24,16},{32,24},{40,32},{48,40},{56,48},{0,56},{9,1},... | collective-permute-start | bytes 15368 | tf_op jit(solution)/shard_map/ppermute | solution.py:22
  34.4 4.1 copy-start.1
  34.4 10.4 %collective-permute-start.3 = (f32[10,1,128]{2,1,0:T(1,128)S(1)}, f32[10,1,128]{2,1,0:T(1,128)S(1)}, u32[]{:S(2)}, u32[]{:S(2)}) collective-permute-start(f32[10,1,128]{2,1,0:T(1,128)S(1)} %pad_maximum_fusion.90), channel_id=1, source_target_pairs={{0,8},{8,16},{16,24},{24,32},{32,40},{40,48},{48,56},{56,0},{1,9},... | collective-permute-start | bytes 15368 | tf_op jit(solution)/shard_map/ppermute | solution.py:20
  36.5 10.8 %collective-permute-start.8 = (f32[10,66,1]{2,1,0:T(8,128)S(1)}, f32[10,66,1]{2,1,0:T(8,128)S(1)}, u32[]{:S(2)}, u32[]{:S(2)}) collective-permute-start(f32[10,66,1]{2,1,0:T(8,128)S(1)} %pad_maximum_fusion.4), channel_id=1, source_target_pairs={{0,1},{1,2},{2,3},{3,4},{4,5},{5,6},{6,7},{7,0},{8,9},{9,10},{10,1... | collective-permute-start | bytes 7928 | tf_op jit(solution)/shard_map/ppermute | solution.py:20
  47.4 7.6 %collective-permute-start.9 = (f32[1,64,128]{2,1,0:T(8,128)S(1)}, f32[1,64,128]{2,1,0:T(8,128)S(1)}, u32[]{:S(2)}, u32[]{:S(2)}) collective-permute-start(f32[1,64,128]{2,1,0:T(8,128)S(1)} %slice.286), channel_id=1, source_target_pairs={{0,64},{64,128},{128,192},{192,256},{256,320},{320,384},{384,448},... | collective-permute-start | bytes 98312 | tf_op jit(solution)/shard_map/ppermute | solution.py:20
  55.0 6.6 collective-permute-start.10
  61.6 11.6 %collective-permute-start.11 = (f32[10,1,128]{2,1,0:T(1,128)S(1)}, f32[10,1,128]{2,1,0:T(1,128)S(1)}, u32[]{:S(2)}, u32[]{:S(2)}) collective-permute-start(f32[10,1,128]{2,1,0:T(1,128)S(1)} %get-tuple-element.28), channel_id=1, source_target_pairs={{0,8},{8,16},{16,24},{24,32},{32,40},{40,48},{48,56},{56,0},{1,9},... | collective-permute-start | bytes 15368 | tf_op jit(solution)/shard_map/ppermute | solution.py:20
  63.6 10.4 %collective-permute-start.12 = (f32[10,1,128]{2,1,0:T(1,128)S(1)}, f32[10,1,128]{2,1,0:T(1,128)S(1)}, u32[]{:S(2)}, u32[]{:S(2)}) collective-permute-start(f32[10,1,128]{2,1,0:T(1,128)S(1)} %get-tuple-element.29), channel_id=1, source_target_pairs={{8,0},{16,8},{24,16},{32,24},{40,32},{48,40},{56,48},{0,56},{9,1},... | collective-permute-start | bytes 15368 | tf_op jit(solution)/shard_map/ppermute | solution.py:22
  74.2 11.6 %collective-permute-start.13 = (f32[10,66,1]{2,1,0:T(8,128)S(1)}, f32[10,66,1]{2,1,0:T(8,128)S(1)}, u32[]{:S(2)}, u32[]{:S(2)}) collective-permute-start(f32[10,66,1]{2,1,0:T(8,128)S(1)} %get-tuple-element.18), channel_id=1, source_target_pairs={{0,1},{1,2},{2,3},{3,4},{4,5},{5,6},{6,7},{7,0},{8,9},{9,10},{10,1... | collective-permute-start | bytes 7928 | tf_op jit(solution)/shard_map/ppermute | solution.py:20
  76.1 10.6 %collective-permute-start.14 = (f32[10,66,1]{2,1,0:T(8,128)S(1)}, f32[10,66,1]{2,1,0:T(8,128)S(1)}, u32[]{:S(2)}, u32[]{:S(2)}) collective-permute-start(f32[10,66,1]{2,1,0:T(8,128)S(1)} %get-tuple-element.19), channel_id=1, source_target_pairs={{1,0},{2,1},{3,2},{4,3},{5,4},{6,5},{7,6},{0,7},{9,8},{10,9},{11,1... | collective-permute-start | bytes 7928 | tf_op jit(solution)/shard_map/ppermute | solution.py:22
  291.6 4.2 collective-permute-start.15
  295.8 6.2 collective-permute-start.16
  302.0 11.4 %collective-permute-start.17 = (f32[10,1,128]{2,1,0:T(1,128)S(1)}, f32[10,1,128]{2,1,0:T(1,128)S(1)}, u32[]{:S(2)}, u32[]{:S(2)}) collective-permute-start(f32[10,1,128]{2,1,0:T(1,128)S(1)} %get-tuple-element.26), channel_id=1, source_target_pairs={{0,8},{8,16},{16,24},{24,32},{32,40},{40,48},{48,56},{56,0},{1,9},... | collective-permute-start | bytes 15368 | tf_op jit(solution)/shard_map/ppermute | solution.py:20
  305.7 8.4 %collective-permute-start.18 = (f32[10,1,128]{2,1,0:T(1,128)S(1)}, f32[10,1,128]{2,1,0:T(1,128)S(1)}, u32[]{:S(2)}, u32[]{:S(2)}) collective-permute-start(f32[10,1,128]{2,1,0:T(1,128)S(1)} %get-tuple-element.27), channel_id=1, source_target_pairs={{8,0},{16,8},{24,16},{32,24},{40,32},{48,40},{56,48},{0,56},{9,1},... | collective-permute-start | bytes 15368 | tf_op jit(solution)/shard_map/ppermute | solution.py:22
  314.3 11.3 %collective-permute-start.19 = (f32[10,66,1]{2,1,0:T(8,128)S(1)}, f32[10,66,1]{2,1,0:T(8,128)S(1)}, u32[]{:S(2)}, u32[]{:S(2)}) collective-permute-start(f32[10,66,1]{2,1,0:T(8,128)S(1)} %get-tuple-element.16), channel_id=1, source_target_pairs={{0,1},{1,2},{2,3},{3,4},{4,5},{5,6},{6,7},{7,0},{8,9},{9,10},{10,1... | collective-permute-start | bytes 7928 | tf_op jit(solution)/shard_map/ppermute | solution.py:20
  316.2 10.3 %collective-permute-start.20 = (f32[10,66,1]{2,1,0:T(8,128)S(1)}, f32[10,66,1]{2,1,0:T(8,128)S(1)}, u32[]{:S(2)}, u32[]{:S(2)}) collective-permute-start(f32[10,66,1]{2,1,0:T(8,128)S(1)} %get-tuple-element.17), channel_id=1, source_target_pairs={{1,0},{2,1},{3,2},{4,3},{5,4},{6,5},{7,6},{0,7},{9,8},{10,9},{11,1... | collective-permute-start | bytes 7928 | tf_op jit(solution)/shard_map/ppermute | solution.py:22
  529.8 3.9 collective-permute-start.21
  533.7 6.5 collective-permute-start.22
  540.2 11.4 %collective-permute-start.23 = (f32[10,1,128]{2,1,0:T(1,128)S(1)}, f32[10,1,128]{2,1,0:T(1,128)S(1)}, u32[]{:S(2)}, u32[]{:S(2)}) collective-permute-start(f32[10,1,128]{2,1,0:T(1,128)S(1)} %get-tuple-element.24), channel_id=1, source_target_pairs={{0,8},{8,16},{16,24},{24,32},{32,40},{40,48},{48,56},{56,0},{1,9},... | collective-permute-start | bytes 15368 | tf_op jit(solution)/shard_map/ppermute | solution.py:20
  543.9 8.4 %collective-permute-start.24 = (f32[10,1,128]{2,1,0:T(1,128)S(1)}, f32[10,1,128]{2,1,0:T(1,128)S(1)}, u32[]{:S(2)}, u32[]{:S(2)}) collective-permute-start(f32[10,1,128]{2,1,0:T(1,128)S(1)} %get-tuple-element.25), channel_id=1, source_target_pairs={{8,0},{16,8},{24,16},{32,24},{40,32},{48,40},{56,48},{0,56},{9,1},... | collective-permute-start | bytes 15368 | tf_op jit(solution)/shard_map/ppermute | solution.py:22
  552.5 11.3 %collective-permute-start.25 = (f32[10,66,1]{2,1,0:T(8,128)S(1)}, f32[10,66,1]{2,1,0:T(8,128)S(1)}, u32[]{:S(2)}, u32[]{:S(2)}) collective-permute-start(f32[10,66,1]{2,1,0:T(8,128)S(1)} %get-tuple-element.14), channel_id=1, source_target_pairs={{0,1},{1,2},{2,3},{3,4},{4,5},{5,6},{6,7},{7,0},{8,9},{9,10},{10,1... | collective-permute-start | bytes 7928 | tf_op jit(solution)/shard_map/ppermute | solution.py:20
  554.9 9.8 %collective-permute-start.26 = (f32[10,66,1]{2,1,0:T(8,128)S(1)}, f32[10,66,1]{2,1,0:T(8,128)S(1)}, u32[]{:S(2)}, u32[]{:S(2)}) collective-permute-start(f32[10,66,1]{2,1,0:T(8,128)S(1)} %get-tuple-element.15), channel_id=1, source_target_pairs={{1,0},{2,1},{3,2},{4,3},{5,4},{6,5},{7,6},{0,7},{9,8},{10,9},{11,1... | collective-permute-start | bytes 7928 | tf_op jit(solution)/shard_map/ppermute | solution.py:22
  672.0 4.6 collective-permute-start.28
  673.9 5.5 collective-permute-start.27
  679.5 11.3 %collective-permute-start.30 = (f32[10,1,128]{2,1,0:T(1,128)S(1)}, f32[10,1,128]{2,1,0:T(1,128)S(1)}, u32[]{:S(2)}, u32[]{:S(2)}) collective-permute-start(f32[10,1,128]{2,1,0:T(1,128)S(1)} %get-tuple-element.22), channel_id=1, source_target_pairs={{0,8},{8,16},{16,24},{24,32},{32,40},{40,48},{48,56},{56,0},{1,9},... | collective-permute-start | bytes 15368 | tf_op jit(solution)/shard_map/ppermute | solution.py:20
  681.4 10.1 %collective-permute-start.29 = (f32[10,1,128]{2,1,0:T(1,128)S(1)}, f32[10,1,128]{2,1,0:T(1,128)S(1)}, u32[]{:S(2)}, u32[]{:S(2)}) collective-permute-start(f32[10,1,128]{2,1,0:T(1,128)S(1)} %get-tuple-element.23), channel_id=1, source_target_pairs={{8,0},{16,8},{24,16},{32,24},{40,32},{48,40},{56,48},{0,56},{9,1},... | collective-permute-start | bytes 15368 | tf_op jit(solution)/shard_map/ppermute | solution.py:22
  691.6 10.0 %collective-permute-start.31 = (f32[10,66,1]{2,1,0:T(8,128)S(1)}, f32[10,66,1]{2,1,0:T(8,128)S(1)}, u32[]{:S(2)}, u32[]{:S(2)}) collective-permute-start(f32[10,66,1]{2,1,0:T(8,128)S(1)} %pad_maximum_fusion), channel_id=1, source_target_pairs={{1,0},{2,1},{3,2},{4,3},{5,4},{6,5},{7,6},{0,7},{9,8},{10,9},{11,1... | collective-permute-start | bytes 7928 | tf_op jit(solution)/shard_map/ppermute | solution.py:22
where the time goes:
time: 709 us; the launch traced here: 703 us
  blocking collectives  504 us (71%)
  starting transfers between devices  138 us (19%)
  waiting for transfers between devices  43.5 us (6%)
  other arithmetic  8.09 us (1%)
  between operations  7.95 us (1%)
    psum x3, blocking collectives, squares(): return lax.psum(jnp.sum(residual * residual), ('ta', 'gx', 'gy'))  294 us
    psum x2, blocking collectives, body(): lax.psum(jnp.sum(direction * applied), ('ta', 'gx', 'gy'))  211 us
    ppermute x15, starting transfers between devices, padded_2(): lax.ppermute(head, axis, [((i + 1) % count, i) for i in range(count)])  91.6 us
    ppermute x17, starting transfers between devices, padded_2(): lax.ppermute(tail, axis, [(i, (i + 1) % count) for i in range(count)])  46.2 us
    ppermute x17, waiting for transfers between devices, padded_2(): lax.ppermute(tail, axis, [(i, (i + 1) % count) for i in range(count)])  26.4 us
    ppermute x15, waiting for transfers between devices, padded_2(): lax.ppermute(head, axis, [((i + 1) % count, i) for i in range(count)])  17.1 us
  transfers between devices with their start and end apart: 32, of which 20 were waited for; matrix products, arithmetic and copies ran while one was open for 0% of the time, Pallas kernels for 0%

commit v1 on v0

v1 whole, which is shorter than its diff:
```python
import functools
import itertools

import jax
import jax.numpy as jnp
from jax import lax
from jax.experimental import pallas as pl
from jax.experimental.pallas import tpu as pltpu
from jax.sharding import PartitionSpec as P

MESH = pl.DeviceIdType.MESH
NEWTON = 6
F32 = jnp.float32
TP, XR, TILES = 13, 72, 9


def roll(v, shift, axis):
    return pltpu.roll(v, shift, axis)


def group_a(c):
    peers = []
    for dz, dc in itertools.product(range(8), range(2)):
        if dz or dc:
            ta = c["ta"] + dc * (1 - 2 * lax.rem(c["ta"], 2))
            peers.append((min(dz, 8 - dz), (ta, c["gx"], lax.rem(c["gy"] + dz, 8))))
    return [p for _, p in sorted(peers, key=lambda e: -e[0])]


def group_b(c):
    y, x = (c["gx"] // 4) * 4 + c["ta"] // 2, lax.rem(c["gx"], 4)
    peers = []
    for dy, dx in itertools.product(range(8), range(4)):
        if dy or dx:
            yy, xx = lax.rem(y + dy, 8), lax.rem(x + dx, 4)
            at = (lax.rem(yy, 4) * 2 + lax.rem(c["ta"], 2), (yy // 4) * 4 + xx, c["gy"])
            peers.append((min(dy, 8 - dy) + min(dx, 4 - dx), at))
    return [p for _, p in sorted(peers, key=lambda e: -e[0])]


def kernel(
    d_hbm, fx_hbm, fy_hbm, c_hbm, i_hbm,
    mo_ref, xo_ref, yo_ref,
    d_ref, fx_ref, fy_ref, c_ref, i_ref, mass, px, py,
    eb, e1, e2, px0, pxm, m0, mm, pyq,
    s_xp, s_xm, s_pp, s_pm, s_mp, s_mm, s_p0, s_m0,
    r_xm, r_xp, r_mm, r_mp, r_pm, r_pp, r_m0, r_p0,
    s_yp, s_ym, r_ym, r_yp, buf_a, buf_b,
    in_sem, ss, rs, ra_send, ra_recv, rb_send, rb_recv,
):
    c = {a: lax.axis_index(a) for a in ("ta", "gx", "gy")}
    ta = c["ta"]
    has_m, has_p = ta > 0, ta < 7
    gxp, gxm = lax.rem(c["gx"] + 1, 8), lax.rem(c["gx"] + 7, 8)
    gyp, gym = lax.rem(c["gy"] + 1, 8), lax.rem(c["gy"] + 7, 8)
    peers_a, peers_b = group_a(c), group_b(c)

    def at(dt, gx):
        return (ta + dt, gx, c["gy"])

    bar = pltpu.get_barrier_semaphore()

    def greet(peer):
        pl.semaphore_signal(bar, inc=1, device_id=peer, device_id_type=MESH)

    for peer in peers_b:
        greet(peer)

    odd = lax.rem(ta, 2) == 1
    away_p = jnp.logical_and(has_p, odd)
    away_m = jnp.logical_and(has_m, jnp.logical_not(odd))

    @pl.when(has_p)
    def _():
        greet(at(1, gxp))
        greet(at(1, gxm))

    @pl.when(has_m)
    def _():
        greet(at(-1, gxp))
        greet(at(-1, gxm))

    @pl.when(away_p)
    def _():
        greet(at(1, c["gx"]))

    @pl.when(away_m)
    def _():
        greet(at(-1, c["gx"]))

    for peer in peers_a:
        greet(peer)

    loads = [
        pltpu.make_async_copy(a, b, in_sem.at[i])
        for i, (a, b) in enumerate(
            ((d_hbm, d_ref), (fx_hbm, fx_ref), (fy_hbm, fy_ref), (c_hbm, c_ref), (i_hbm, i_ref))
        )
    ]
    for copy in loads:
        copy.start()
    for copy in loads:
        copy.wait()

    lane64 = lax.broadcasted_iota(jnp.int32, (64, 128), 1)
    row64 = lax.broadcasted_iota(jnp.int32, (64, 128), 0)
    lane8 = lax.broadcasted_iota(jnp.int32, (8, 128), 1)
    sub8 = lax.broadcasted_iota(jnp.int32, (8, 128), 0)

    def newton(t, carry):
        before, packed = carry
        d, fx, fy = d_ref[t], fx_ref[t], fy_ref[t]
        q = fx * fx + fy * fy
        a = 1.0 + c_ref[t]
        m = (d + 0.5 * q) / (a + q)
        for _ in range(NEWTON - 1):
            s = m + 1.0
            s3 = s * s * s
            m = (d * s3 + q * (1.5 * s - 1.0)) / (a * s3 + q)
        shrink = m / (m + 1.0)
        vx, vy = fx * shrink, fy * shrink
        mass[t] = m
        px[t] = vx
        py[t] = vy
        b = m - before
        b = b + vx - jnp.where(row64 == 0, 0.0, roll(vx, 1, 0))
        b = b + vy - jnp.where(lane64 == 0, 0.0, roll(vy, 1, 1))
        eb[t + 2, 0:64, :] = b
        px0[pl.ds(t + 2, 1), :] = vx[63:64]
        for tile in range(8):
            k = t * TILES + tile
            packed = jnp.where(
                lane8 == k, roll(vy[8 * tile : 8 * tile + 8], k + 1, 1), packed
            )
        return m, packed

    start = jnp.where(ta == 0, i_ref[...], 0.0)
    m7, py127 = lax.fori_loop(0, 8, newton, (start, jnp.zeros((8, 128), F32)))

    for t in range(8):
        s_xp[2 * t : 2 * t + 2, :] = eb[t + 2, 62:64, :]
        s_xm[3 * t : 3 * t + 3, :] = eb[t + 2, 0:3, :]
    s_xp[16:24, :] = px0[2:10, :]
    s_xp[24:26, :] = m7[62:64]
    s_xp[26:28, :] = py127[6:8]
    s_xm[24:27, :] = m7[0:3]
    s_xm[27:30, :] = py127[0:3]
    for j in range(2):
        s_pp[2 * j : 2 * j + 2, :] = eb[8 + j, 62:64, :]
        s_pm[3 * j : 3 * j + 3, :] = eb[8 + j, 0:3, :]
    s_pp[4:6, :] = px0[8:10, :]
    s_pp[6:8, :] = m7[62:64]
    s_pp[8:10, :] = py127[6:8]
    s_pm[6:9, :] = m7[0:3]
    s_pm[9:12, :] = py127[0:3]
    for j in range(3):
        s_mp[2 * j : 2 * j + 2, :] = eb[2 + j, 62:64, :]
        s_mm[3 * j : 3 * j + 3, :] = eb[2 + j, 0:3, :]
    s_mp[6:9, :] = px0[2:5, :]
    s_mp[9:11, :] = py127[6:8]
    s_mm[9:12, :] = py127[0:3]
    s_p0[0:8, :] = py127
    s_p0[8:10, :] = px0[8:10, :]
    s_m0[0:8, :] = py127
    s_m0[8:11, :] = px0[2:5, :]

    def one(flag):
        return jnp.where(flag, 1, 0)

    greeted = len(peers_a) + len(peers_b) + 2 * one(has_p) + 2 * one(has_m)
    pl.semaphore_wait(bar, greeted + one(away_p) + one(away_m))

    def remote(i, src, dst, peer):
        return pltpu.make_async_remote_copy(
            src_ref=src, dst_ref=dst, send_sem=ss.at[i], recv_sem=rs.at[i],
            device_id=peer, device_id_type=MESH,
        )

    x_p = remote(0, s_xp, r_xm, at(0, gxp))
    x_m = remote(1, s_xm, r_xp, at(0, gxm))
    t_p = [
        remote(2, s_pp, r_mm, at(1, gxp)),
        remote(3, s_pm, r_mp, at(1, gxm)),
        remote(4, s_p0, r_m0, at(1, c["gx"])),
        remote(5, eb.at[8:10, 0:64], eb.at[0:2, 0:64], at(1, c["gx"])),
        remote(6, mass.at[7], mm.at[0:64], at(1, c["gx"])),
    ]
    t_m = [
        remote(7, s_mp, r_pm, at(-1, gxp)),
        remote(8, s_mm, r_pp, at(-1, gxm)),
        remote(9, s_m0, r_p0, at(-1, c["gx"])),
        remote(10, eb.at[2:5, 0:64], eb.at[10:13, 0:64], at(-1, c["gx"])),
    ]

    @pl.when(has_p)
    def _():
        for copy in t_p[:2]:
            copy.start()

    @pl.when(has_m)
    def _():
        for copy in t_m[:2]:
            copy.start()

    x_p.start()
    x_m.start()

    @pl.when(has_m)
    def _():
        for copy in t_m[2:]:
            copy.start()

    @pl.when(has_p)
    def _():
        for copy in t_p[2:]:
            copy.start()

    m0[0:64, :] = m7

    x_p.wait()
    x_m.wait()

    @pl.when(has_p)
    def _():
        for copy in t_p:
            copy.wait_send()

    @pl.when(has_m)
    def _():
        for copy in t_m:
            copy.wait_send()

    for t in range(8):
        eb[t + 2, 64:67, :] = r_xp[3 * t : 3 * t + 3, :]
        eb[t + 2, 70:72, :] = r_xm[2 * t : 2 * t + 2, :]
    pxm[2:10, :] = r_xm[16:24, :]
    m0[64:67, :] = r_xp[24:27, :]
    m0[70:72, :] = r_xm[24:26, :]
    pyq[0, 0:3, :] = r_xp[27:30, :]
    pyq[0, 6:8, :] = r_xm[26:28, :]

    @pl.when(has_m)
    def _():
        for copy in t_p:
            copy.wait_recv()
        for j in range(2):
            eb[j, 64:67, :] = r_mp[3 * j : 3 * j + 3, :]
            eb[j, 70:72, :] = r_mm[2 * j : 2 * j + 2, :]
        pxm[0:2, :] = r_mm[4:6, :]
        px0[0:2, :] = r_m0[8:10, :]
        mm[64:67, :] = r_mp[6:9, :]
        mm[70:72, :] = r_mm[6:8, :]
        pyq[1, 0:3, :] = r_mp[9:12, :]
        pyq[1, 6:8, :] = r_mm[8:10, :]
        eb[2] = eb[2] - mm[...]

    @pl.when(has_p)
    def _():
        for copy in t_m:
            copy.wait_recv()
        for j in range(3):
            eb[10 + j, 64:67, :] = r_pp[3 * j : 3 * j + 3, :]
            eb[10 + j, 70:72, :] = r_pm[2 * j : 2 * j + 2, :]
        pxm[10:13, :] = r_pm[6:9, :]
        px0[10:13, :] = r_p0[8:11, :]
        pyq[2, 0:3, :] = r_pp[9:12, :]
        pyq[2, 6:8, :] = r_pm[9:11, :]
        eb[10] = eb[10] - m0[...]

    for p in range(TP):
        eb[p, 0:1, :] = eb[p, 0:1, :] - pxm[p : p + 1, :]
        eb[p, 64:65, :] = eb[p, 64:65, :] - px0[p : p + 1, :]

    tile_of, plane_of = lax.rem(lane8, TILES), lane8 // TILES

    def side(i, low, high):
        v = pyq[i]
        return jnp.where(sub8 < 4, roll(v, low, 1), roll(v, high, 1))

    pyo = jnp.where(tile_of == 8, side(0, 26, 19), roll(py127, 18, 1))
    pyl = jnp.where(tile_of == 8, side(1, 82, 75), roll(r_m0[0:8, :], 74, 1))
    pyh = jnp.where(tile_of == 8, side(2, 98, 91), roll(r_p0[0:8, :], 90, 1))
    mirror_l = jnp.where(plane_of == 1, roll(pyo, 119, 1), roll(pyo, 101, 1))
    mirror_h = jnp.where(plane_of == 11, -roll(pyo, 18, 1), -roll(pyo, 36, 1))
    mirror_h = jnp.where(plane_of == 10, 0.0, mirror_h)
    pyl = jnp.where(has_m, pyl, mirror_l)
    pyh = jnp.where(has_p, pyh, mirror_h)
    py0 = jnp.where(plane_of < 2, pyl, jnp.where(plane_of < 10, pyo, pyh))

    @pl.when(jnp.logical_not(has_m))
    def _():
        eb[1] = eb[2]
        eb[0] = eb[3]

    @pl.when(jnp.logical_not(has_p))
    def _():
        eb[10] = jnp.zeros((XR, 128), F32)
        eb[11] = -eb[9]
        eb[12] = -eb[8]

    def pack(p, cols):
        v = eb[p]
        new = []
        for col, packed in zip((126, 127, 0, 1, 2), cols):
            for tile in range(TILES):
                k = p * TILES + tile
                r = roll(v[8 * tile : 8 * tile + 8], lax.rem(k + 128 - col, 128), 1)
                packed = jnp.where(lane8 == k, r, packed)
            new.append(packed)
        return tuple(new)

    zero8 = jnp.zeros((8, 128), F32)
    b126, b127, b0, b1, b2 = lax.fori_loop(0, TP, pack, (zero8,) * 5)
    s_yp[0:8, :] = b126
    s_yp[8:16, :] = b127
    s_yp[16:24, :] = py0
    s_ym[0:8, :] = b0
    s_ym[8:16, :] = b1
    s_ym[16:24, :] = b2
    y_p = remote(11, s_yp, r_ym, (ta, c["gx"], gyp))
    y_m = remote(12, s_ym, r_yp, (ta, c["gx"], gym))
    y_p.start()
    y_m.start()
    y_p.wait()
    y_m.wait()
    bm2, bm1, pym = r_ym[0:8, :], r_ym[8:16, :], r_ym[16:24, :]
    b128, b129, b130 = r_yp[0:8, :] - py0, r_yp[8:16, :], r_yp[16:24, :]
    b0 = b0 - pym

    def around(v):
        up = roll(v, 7, 0)
        nxt = jnp.where(tile_of == 8, roll(up, 8, 1), roll(up, 127, 1))
        up = jnp.where(sub8 == 7, nxt, up)
        down = roll(v, 1, 0)
        prv = jnp.where(tile_of == 0, roll(down, 120, 1), roll(down, 1, 1))
        down = jnp.where(sub8 == 0, prv, down)
        return (roll(v, 9, 1) + roll(v, 119, 1)) + (down + up)

    um1 = around(bm1) + (bm2 + b0)
    u127 = around(b127) + (b126 + b128)
    u128 = around(b128) + (b127 + b129)
    u129 = around(b129) + (b128 + b130)
    w128 = around(u128) + (u127 + u129)

    lane72 = lax.broadcasted_iota(jnp.int32, (XR, 128), 1)

    def unpack(packed, p, lane, tiles):
        return jnp.concatenate(
            [roll(packed, lax.rem(128 + lane - p * TILES - t, 128), 1) for t in range(tiles)], 0
        )

    def fix(p, _):
        eb[p] = jnp.where(lane72 == 0, unpack(b0, p, 0, TILES), eb[p])
        return 0

    lax.fori_loop(0, TP, fix, 0)

    def spread(src, dst, left, right):
        def step(p, _):
            v = src[p]
            lo = jnp.where(lane72 == 0, unpack(left, p, 0, TILES), roll(v, 1, 1))
            hi = jnp.where(lane72 == 127, unpack(right, p, 127, TILES), roll(v, 127, 1))
            dst[p] = (src[p - 1] + src[p + 1]) + (roll(v, 1, 0) + roll(v, XR - 1, 0)) + (lo + hi)
            return 0

        return step

    lax.fori_loop(1, 12, spread(eb, e1, bm1, b128), 0)
    lax.fori_loop(2, 11, spread(e1, e2, um1, u128), 0)

    def fold(v):
        return jnp.sum(v.reshape(8, 8, 128), axis=0)

    def moments(p, acc):
        b, u, full = eb[p, 0:64, :], e1[p, 0:64, :], e2[p]
        w = full[0:64]
        hi = jnp.where(lane64 == 127, unpack(w128, p, 127, 8), roll(w, 127, 1))
        later = (e2[p + 1, 0:64, :] + roll(full, XR - 1, 0)[0:64]) + hi
        terms = (b * b, b * u, u * u, u * w, w * w, w * later)
        return tuple(a + fold(v) for a, v in zip(acc, terms))

    acc = lax.fori_loop(2, 10, moments, (zero8,) * 6)
    w0 = e2[2, 0:64, :]
    first = jnp.where(ta == 0, fold(w0 * w0), 0.0)
    acc = acc[:5] + (2.0 * acc[5] + first,)
    lane1 = lax.broadcasted_iota(jnp.int32, (1, 128), 1)
    row = jnp.zeros((1, 128), F32)
    for i, v in enumerate(acc):
        row = jnp.where(lane1 == i, jnp.sum(v, keepdims=True), row)

    def all_sum(buf, row, peers, send, recv):
        n = len(peers)
        buf[0] = row
        for i, peer in enumerate(peers):
            pltpu.make_async_remote_copy(
                src_ref=buf.at[0], dst_ref=buf.at[i + 1], send_sem=send, recv_sem=recv,
                device_id=peer, device_id_type=MESH,
            ).start()
        rest = pltpu.make_async_remote_copy(
            src_ref=buf.at[1 : n + 1], dst_ref=buf.at[1 : n + 1], send_sem=send, recv_sem=recv,
            device_id=peers[0], device_id_type=MESH,
        )
        rest.wait_recv()
        total = buf[0]
        for i in range(n):
            total = total + buf[i + 1]
        return total, rest

    row, sent_a = all_sum(buf_a, row, peers_a, ra_send, ra_recv)
    row, sent_b = all_sum(buf_b, row, peers_b, rb_send, rb_recv)
    n = [jnp.sum(jnp.where(lane1 == i, row, 0.0), axis=1, keepdims=True) for i in range(6)]

    g0, g1, g2, g3, g4 = (6.0 * n[i] - n[i + 1] for i in range(5))
    l1, l2 = g1 / g0, g2 / g0
    d1 = g2 - l1 * g1
    f1 = g3 - l2 * g1
    l3 = f1 / d1
    d2 = g4 - l2 * g2 - l3 * f1
    y1 = n[1] - l1 * n[0]
    y2 = n[2] - l2 * n[0] - l3 * y1
    c2 = y2 / d2
    c1 = y1 / d1 - l3 * c2
    c0 = n[0] / g0 - l1 * c1 - l2 * c2
    c0, c1, c2 = (jnp.broadcast_to(v, (8, 128)) for v in (c0, c1, c2))
    k0, k1, k2 = (jnp.broadcast_to(v[0:1], (XR, 128)) for v in (c0, c1, c2))

    v128 = c0 * b128 + c1 * u128 + c2 * w128

    def plane(p):
        return k0 * eb[p] + k1 * e1[p] + k2 * e2[p]

    def finish(t, v):
        p = t + 2
        nxt = plane(p + 1)
        v64 = v[0:64]
        hi = jnp.where(lane64 == 127, unpack(v128, p, 127, 8), roll(v64, 127, 1))
        mo_ref[t] = mass[t] - (v64 - nxt[0:64])
        xo_ref[t] = px[t] - (v64 - roll(v, XR - 1, 0)[0:64])
        yo_ref[t] = py[t] - (v64 - hi)
        return nxt

    lax.fori_loop(0, 8, finish, plane(2))
    sent_a.wait_send()
    sent_b.wait_send()


def body(density, flux_x, flux_y, congestion, initial_density):
    block = jax.ShapeDtypeStruct((8, 64, 128), F32)
    vm = lambda *s: pltpu.VMEM(s, F32)
    dma = pltpu.SemaphoreType.DMA
    return pl.pallas_call(
        kernel,
        out_shape=(block,) * 3,
        in_specs=[pl.BlockSpec(memory_space=pl.ANY)] * 5,
        out_specs=[pl.BlockSpec(memory_space=pltpu.VMEM)] * 3,
        scratch_shapes=[vm(8, 64, 128)] * 4
        + [vm(64, 128)]
        + [vm(8, 64, 128)] * 3
        + [vm(TP, XR, 128)] * 3
        + [vm(16, 128)] * 2
        + [vm(XR, 128)] * 2
        + [vm(3, 8, 128)]
        + [vm(32, 128)] * 2
        + [vm(16, 128)] * 6
        + [vm(32, 128)] * 2
        + [vm(16, 128)] * 6
        + [vm(24, 128)] * 4
        + [vm(16, 1, 128), vm(32, 1, 128)]
        + [dma((5,)), dma((13,)), dma((13,))]
        + [dma] * 4,
        compiler_params=pltpu.CompilerParams(collective_id=0, has_side_effects=True),
        name="prox_project",
    )(density, flux_x, flux_y, congestion, initial_density)


def solution(mesh):
    spec = P("ta", "gx", "gy")
    return jax.shard_map(
        body,
        mesh=mesh,
        in_specs=(spec,) * 4 + (P("gx", "gy"),),
        out_specs=(spec,) * 3,
        check_vma=False,
    )
```

time: 709 us -> 47.4 us (0.07)
  blocking collectives: 504 us -> 0 us
  starting transfers between devices: 138 us -> 0 us
  waiting for transfers between devices: 43.5 us -> 0 us
  Pallas kernels: 0 us -> 43.1 us
  other arithmetic: 8.09 us -> 0 us
  between operations: 7.95 us -> 0.65 us
    psum x5 -> x0, blocking collectives: 504 us -> none  [the longest x3 294 us: squares(): return lax.psum(jnp.sum(residual * residual), ('ta', 'gx', 'gy'))]
    ppermute x32 -> x0, starting transfers between devices: 138 us -> none  [the longest x15 91.6 us: padded_2(): lax.ppermute(head, axis, [((i + 1) % count, i) for i in range(count)])]
    ppermute x32 -> x0, waiting for transfers between devices: 43.5 us -> none  [the longest x17 26.4 us: padded_2(): lax.ppermute(tail, axis, [(i, (i + 1) % count) for i in range(count)])]
    pallas_call x0 -> x1, Pallas kernels: none -> 43.1 us  [body(): pl.pallas_call(kernel, out_shape=(block,) * 3, in_specs=[pl.BlockSpec(mem...]
  transfers between devices with their start and end apart: 32 -> 0, of which waited for: 20 -> 0; matrix products, arithmetic and copies ran while one was open for 0% -> 0% of each run, Pallas kernels for 0% -> 0%
where the time goes in v1:
time: 47.4 us; the launch traced here: 47.2 us
  Pallas kernels  43.1 us (91%)
  local copies, waits for them, and re-layouts  3.46 us (7%)
  between operations  0.65 us (1%)
    pallas_call x1, Pallas kernels, body(): pl.pallas_call(kernel, out_shape=(block,) * 3, in_specs=[pl.BlockSpec(mem...  43.1 us
    unnamed x7, local copies, waits for them, and re-layouts  3.46 us

profile of v1, /device:TPU:1, one launch (start us, length us, event | category | flops | bytes accessed | tf_op | source)
XLA Modules:
  0.0 47.2 jit_solution(16746295800000814020)
XLA Ops:
  0.6 43.1 %prox_project.1 = (f32[8,64,128]{2,1,0:T(8,128)}, f32[8,64,128]{2,1,0:T(8,128)}, f32[8,64,128]{2,1,0:T(8,128)}) custom-call(f32[8,64,128]{2,1,0:T(8,128)} %d_hbm.1, f32[8,64,128]{2,1,0:T(8,128)} %fx_hbm.1, f32[8,64,128]{2,1,0:T(8,128)} %fy_hbm.1, f32[8,64,128]{2,1,0:T(8,128)} %c_hbm.1, f32[64,128]{1,0:T(8,128)} %i_hbm.1), custom_call_target="tpu_custom_call" | custom-call | tf_op jit(solution)/shard_map/prox_project/pallas_call | solution.py:451
  43.7 0.0 copy-start.1
  43.7 1.7 %copy.11 = f32[8,64,128]{2,1,0:T(8,128)} copy(f32[8,64,128]{2,1,0:T(8,128)} %get-tuple-element.6) | data formatting | bytes 524288
  45.5 0.0 copy-done.1
  45.5 0.0 copy-start
  45.5 0.7 %copy.12 = f32[8,64,128]{2,1,0:T(8,128)} copy(f32[8,64,128]{2,1,0:T(8,128)S(1)} %copy-done.1) | data formatting | bytes 524288
  46.2 0.3 copy-done
  46.5 0.7 %copy.13 = f32[8,64,128]{2,1,0:T(8,128)} copy(f32[8,64,128]{2,1,0:T(8,128)S(1)} %copy-done) | data formatting | bytes 524288
Async XLA Ops:
  43.7 1.7 %copy-start.1 = (f32[8,64,128]{2,1,0:T(8,128)S(1)}, f32[8,64,128]{2,1,0:T(8,128)}, u32[]{:S(2)}) copy-start(f32[8,64,128]{2,1,0:T(8,128)} %get-tuple-element.7) | copy-start | bytes 786436
  45.5 1.0 %copy-start = (f32[8,64,128]{2,1,0:T(8,128)S(1)}, f32[8,64,128]{2,1,0:T(8,128)}, u32[]{:S(2)}) copy-start(f32[8,64,128]{2,1,0:T(8,128)} %get-tuple-element.8) | copy-start | bytes 786436

commit v2 on v1

v2 whole, which is shorter than its diff:
```python
import functools
import itertools

import jax
import jax.numpy as jnp
from jax import lax
from jax.experimental import pallas as pl
from jax.experimental.pallas import tpu as pltpu
from jax.sharding import PartitionSpec as P

MESH = pl.DeviceIdType.MESH
NEWTON = 6
F32 = jnp.float32
TP, XR = 13, 72
VMEM_MAIN, VMEM_STORE = 16 * 2**20, 2**20


def roll(v, shift, axis):
    return pltpu.roll(v, shift, axis)


def group_a(c):
    peers = []
    for dz, dc in itertools.product(range(8), range(2)):
        if dz or dc:
            ta = c["ta"] + dc * (1 - 2 * lax.rem(c["ta"], 2))
            peers.append((min(dz, 8 - dz), (ta, c["gx"], lax.rem(c["gy"] + dz, 8))))
    return [p for _, p in sorted(peers, key=lambda e: -e[0])]


def group_b(c):
    y, x = (c["gx"] // 4) * 4 + c["ta"] // 2, lax.rem(c["gx"], 4)
    peers = []
    for dy, dx in itertools.product(range(8), range(4)):
        if dy or dx:
            yy, xx = lax.rem(y + dy, 8), lax.rem(x + dx, 4)
            at = (lax.rem(yy, 4) * 2 + lax.rem(c["ta"], 2), (yy // 4) * 4 + xx, c["gy"])
            peers.append((min(dy, 8 - dy) + min(dx, 4 - dx), at))
    return [p for _, p in sorted(peers, key=lambda e: -e[0])]


def kernel(
    d_hbm, fx_hbm, fy_hbm, c_hbm, i_hbm,
    mo_ref, xo_ref, yo_ref,
    d_ref, fx_ref, fy_ref, c_ref, i_ref, mass, px, py,
    eb, e1, e2, px0, pxm, m0, mm, pyo, pyl, pyh, diffs,
    s_xp, s_xm, s_pp, s_pm, s_mp, s_mm,
    r_xm, r_xp, r_mm, r_mp, r_pm, r_pp,
    s_yp, s_ym, r_ym, r_yp, buf_a, buf_b,
    in_sem, ss, rs, ra_send, ra_recv, rb_send, rb_recv,
):
    c = {a: lax.axis_index(a) for a in ("ta", "gx", "gy")}
    ta = c["ta"]
    has_m, has_p = ta > 0, ta < 7
    gxp, gxm = lax.rem(c["gx"] + 1, 8), lax.rem(c["gx"] + 7, 8)
    gyp, gym = lax.rem(c["gy"] + 1, 8), lax.rem(c["gy"] + 7, 8)
    peers_a, peers_b = group_a(c), group_b(c)

    def at(dt, gx):
        return (ta + dt, gx, c["gy"])

    bar = pltpu.get_barrier_semaphore()

    def greet(peer):
        pl.semaphore_signal(bar, inc=1, device_id=peer, device_id_type=MESH)

    for peer in peers_b:
        greet(peer)

    odd = lax.rem(ta, 2) == 1
    away_p = jnp.logical_and(has_p, odd)
    away_m = jnp.logical_and(has_m, jnp.logical_not(odd))

    @pl.when(has_p)
    def _():
        greet(at(1, gxp))
        greet(at(1, gxm))

    @pl.when(has_m)
    def _():
        greet(at(-1, gxp))
        greet(at(-1, gxm))

    @pl.when(away_p)
    def _():
        greet(at(1, c["gx"]))

    @pl.when(away_m)
    def _():
        greet(at(-1, c["gx"]))

    for peer in peers_a:
        greet(peer)

    loads = [
        pltpu.make_async_copy(a, b, in_sem.at[i])
        for i, (a, b) in enumerate(
            ((d_hbm, d_ref), (fx_hbm, fx_ref), (fy_hbm, fy_ref), (c_hbm, c_ref), (i_hbm, i_ref))
        )
    ]
    for copy in loads:
        copy.start()
    for copy in loads:
        copy.wait()

    lane64 = lax.broadcasted_iota(jnp.int32, (64, 128), 1)
    row64 = lax.broadcasted_iota(jnp.int32, (64, 128), 0)
    lane8 = lax.broadcasted_iota(jnp.int32, (8, 128), 1)
    lane72 = lax.broadcasted_iota(jnp.int32, (XR, 128), 1)
    slot8, plane8 = lax.rem(lane8, 8), lane8 // 8
    slot72 = lax.rem(lane72, 8)
    pyo[...] = jnp.zeros((XR, 128), F32)

    def newton(t, before):
        d, fx, fy = d_ref[t], fx_ref[t], fy_ref[t]
        q = fx * fx + fy * fy
        a = 1.0 + c_ref[t]
        m = (d + 0.5 * q) / (a + q)
        for _ in range(NEWTON - 1):
            s = m + 1.0
            s3 = s * s * s
            m = (d * s3 + q * (1.5 * s - 1.0)) / (a * s3 + q)
        shrink = m / (m + 1.0)
        vx, vy = fx * shrink, fy * shrink
        mass[t] = m
        px[t] = vx
        py[t] = vy
        b = m - before
        b = b + vx - jnp.where(row64 == 0, 0.0, roll(vx, 1, 0))
        b = b + vy - jnp.where(lane64 == 0, 0.0, roll(vy, 1, 1))
        eb[t + 2, 0:64, :] = b
        px0[pl.ds(t + 2, 1), :] = vx[63:64]
        pyo[0:64, :] = jnp.where(lane64 == 8 * t + 21, roll(vy, 8 * t + 22, 1), pyo[0:64, :])
        return m

    start = jnp.where(ta == 0, i_ref[...], 0.0)
    m7 = lax.fori_loop(0, 8, newton, start)

    for t in range(8):
        s_xp[2 * t : 2 * t + 2, :] = eb[t + 2, 62:64, :]
        s_xm[3 * t : 3 * t + 3, :] = eb[t + 2, 0:3, :]
    s_xp[16:24, :] = px0[2:10, :]
    s_xp[24:26, :] = m7[62:64]
    s_xp[26:28, :] = pyo[62:64, :]
    s_xm[24:27, :] = m7[0:3]
    s_xm[27:30, :] = pyo[0:3, :]
    for j in range(2):
        s_pp[2 * j : 2 * j + 2, :] = eb[8 + j, 62:64, :]
        s_pm[3 * j : 3 * j + 3, :] = eb[8 + j, 0:3, :]
    s_pp[4:6, :] = px0[8:10, :]
    s_pp[6:8, :] = m7[62:64]
    s_pp[8:10, :] = pyo[62:64, :]
    s_pm[6:9, :] = m7[0:3]
    s_pm[9:12, :] = pyo[0:3, :]
    for j in range(3):
        s_mp[2 * j : 2 * j + 2, :] = eb[2 + j, 62:64, :]
        s_mm[3 * j : 3 * j + 3, :] = eb[2 + j, 0:3, :]
    s_mp[6:9, :] = px0[2:5, :]
    s_mp[9:11, :] = pyo[62:64, :]
    s_mm[9:12, :] = pyo[0:3, :]
    def one(flag):
        return jnp.where(flag, 1, 0)

    greeted = len(peers_a) + len(peers_b) + 2 * one(has_p) + 2 * one(has_m)
    pl.semaphore_wait(bar, greeted + one(away_p) + one(away_m))

    def remote(i, src, dst, peer):
        return pltpu.make_async_remote_copy(
            src_ref=src, dst_ref=dst, send_sem=ss.at[i], recv_sem=rs.at[i],
            device_id=peer, device_id_type=MESH,
        )

    x_p = remote(0, s_xp, r_xm, at(0, gxp))
    x_m = remote(1, s_xm, r_xp, at(0, gxm))
    t_p = [
        remote(2, s_pp, r_mm, at(1, gxp)),
        remote(3, s_pm, r_mp, at(1, gxm)),
        remote(4, px0.at[8:10], px0.at[0:2], at(1, c["gx"])),
        remote(5, eb.at[8:10, 0:64], eb.at[0:2, 0:64], at(1, c["gx"])),
        remote(6, mass.at[7], mm.at[0:64], at(1, c["gx"])),
        remote(7, pyo.at[0:64], pyl.at[0:64], at(1, c["gx"])),
    ]
    t_m = [
        remote(8, s_mp, r_pm, at(-1, gxp)),
        remote(9, s_mm, r_pp, at(-1, gxm)),
        remote(10, px0.at[2:5], px0.at[10:13], at(-1, c["gx"])),
        remote(11, eb.at[2:5, 0:64], eb.at[10:13, 0:64], at(-1, c["gx"])),
        remote(12, pyo.at[0:64], pyh.at[0:64], at(-1, c["gx"])),
    ]

    @pl.when(has_p)
    def _():
        for copy in t_p[:2]:
            copy.start()

    @pl.when(has_m)
    def _():
        for copy in t_m[:2]:
            copy.start()

    x_p.start()
    x_m.start()

    @pl.when(has_m)
    def _():
        for copy in t_m[2:]:
            copy.start()

    @pl.when(has_p)
    def _():
        for copy in t_p[2:]:
            copy.start()

    m0[0:64, :] = m7

    x_p.wait()
    x_m.wait()

    @pl.when(has_p)
    def _():
        for copy in t_p:
            copy.wait_send()

    @pl.when(has_m)
    def _():
        for copy in t_m:
            copy.wait_send()

    for t in range(8):
        eb[t + 2, 64:67, :] = r_xp[3 * t : 3 * t + 3, :]
        eb[t + 2, 70:72, :] = r_xm[2 * t : 2 * t + 2, :]
    pxm[2:10, :] = r_xm[16:24, :]
    m0[64:67, :] = r_xp[24:27, :]
    m0[70:72, :] = r_xm[24:26, :]
    pyo[64:67, :] = r_xp[27:30, :]
    pyo[70:72, :] = r_xm[26:28, :]

    @pl.when(has_m)
    def _():
        for copy in t_p:
            copy.wait_recv()
        for j in range(2):
            eb[j, 64:67, :] = r_mp[3 * j : 3 * j + 3, :]
            eb[j, 70:72, :] = r_mm[2 * j : 2 * j + 2, :]
        pxm[0:2, :] = r_mm[4:6, :]
        mm[64:67, :] = r_mp[6:9, :]
        mm[70:72, :] = r_mm[6:8, :]
        pyl[64:67, :] = r_mp[9:12, :]
        pyl[70:72, :] = r_mm[8:10, :]
        eb[2] = eb[2] - mm[...]

    @pl.when(has_p)
    def _():
        for copy in t_m:
            copy.wait_recv()
        for j in range(3):
            eb[10 + j, 64:67, :] = r_pp[3 * j : 3 * j + 3, :]
            eb[10 + j, 70:72, :] = r_pm[2 * j : 2 * j + 2, :]
        pxm[10:13, :] = r_pm[6:9, :]
        pyh[64:67, :] = r_pp[9:12, :]
        pyh[70:72, :] = r_pm[9:11, :]
        eb[10] = eb[10] - m0[...]

    for p in range(TP):
        eb[p, 0:1, :] = eb[p, 0:1, :] - pxm[p : p + 1, :]
        eb[p, 64:65, :] = eb[p, 64:65, :] - px0[p : p + 1, :]

    own = pyo[...]
    low = jnp.where(lane72 < 8, roll(own, 104, 1), roll(own, 120, 1))
    high = jnp.where(lane72 < 96, -roll(own, 16, 1), -roll(own, 32, 1))
    high = jnp.where(lane72 < 88, 0.0, high)
    low = jnp.where(has_m, roll(pyl[...], 64, 1), low)
    high = jnp.where(has_p, roll(pyh[...], 64, 1), high)
    py0 = jnp.where(lane72 < 16, low, jnp.where(lane72 < 80, own, high))

    @pl.when(jnp.logical_not(has_m))
    def _():
        eb[1] = eb[2]
        eb[0] = eb[3]

    @pl.when(jnp.logical_not(has_p))
    def _():
        eb[10] = jnp.zeros((XR, 128), F32)
        eb[11] = -eb[9]
        eb[12] = -eb[8]

    def pack(p, strips):
        v = eb[p]
        here = lane72 // 8 == p
        shifted = (roll(v, 8 * p + 2, 1), roll(v, 8 * p + 5, 1))
        return tuple(jnp.where(here, r, strip) for r, strip in zip(shifted, strips))

    zero8, zero72 = jnp.zeros((8, 128), F32), jnp.zeros((XR, 128), F32)
    left, right = lax.fori_loop(0, TP, pack, (zero72, zero72))
    s_yp[...] = jnp.where(slot72 == 5, py0, right)
    s_ym[...] = left
    y_p = remote(13, s_yp, r_ym, (ta, c["gx"], gyp))
    y_m = remote(14, s_ym, r_yp, (ta, c["gx"], gym))
    y_p.start()
    y_m.start()

    def spread(src, dst):
        def step(p, _):
            v = src[p]
            ends = roll(v, 1, 1) + roll(v, 127, 1)
            dst[p] = (src[p - 1] + src[p + 1]) + (roll(v, 1, 0) + roll(v, XR - 1, 0)) + ends
            return 0

        return step

    def fold(v):
        return jnp.sum(v.reshape(8, 8, 128), axis=0)

    def moments(p, acc):
        b, u, full = eb[p, 0:64, :], e1[p, 0:64, :], e2[p]
        w = full[0:64]
        later = e2[p + 1, 0:64, :] + roll(full, XR - 1, 0)[0:64]
        terms = (b * b, b * u, u * u, u * w, w * w, w * later, w * roll(w, 127, 1))
        return tuple(a + fold(v) for a, v in zip(acc, terms))

    lax.fori_loop(1, 12, spread(eb, e1), 0)
    lax.fori_loop(2, 11, spread(e1, e2), 0)
    acc = lax.fori_loop(2, 10, moments, (zero8,) * 7)
    w0 = e2[2, 0:64, :]
    first = fold(w0 * w0)

    y_p.wait()
    y_m.wait()
    near = roll(r_ym[...], 125, 1)
    left = jnp.where(slot72 < 2, near, left) - jnp.where(slot72 == 2, near, 0.0)
    near = roll(r_yp[...], 3, 1)
    right = jnp.where(slot72 >= 5, near, right) - jnp.where(slot72 == 5, py0, 0.0)

    def around(v):
        return (
            (roll(v, 8, 1) + roll(v, 120, 1))
            + (roll(v, 1, 0) + roll(v, XR - 1, 0))
            + (roll(v, 1, 1) + roll(v, 127, 1))
        )

    strips = []
    inner = jnp.logical_and(lane8 >= 3, lane8 < 126)
    acc = [jnp.where(inner, v, 0.0) for v in acc[:6]] + [jnp.where(lane8 == 125, 0.0, jnp.where(inner, acc[6], 0.0))]
    first = jnp.where(inner, first, 0.0)
    block = jnp.logical_and(plane8 >= 2, plane8 < 10)
    for v, lo, hi in ((left, 2, 5), (right, 3, 5)):
        u = around(v)
        w = around(u)
        strips.append((v, u, w))
        later = (roll(w, 120, 1) + roll(w, XR - 1, 0))[0:64]
        v, u, w = v[0:64], u[0:64], w[0:64]
        cells = jnp.logical_and(block, jnp.logical_and(slot8 >= lo, slot8 < hi))
        pairs = jnp.logical_and(block, jnp.logical_and(slot8 >= 2, slot8 < 5))
        ww = fold(w * w)
        terms = [fold(e) for e in (v * v, v * u, u * u, u * w)] + [ww, fold(w * later)]
        acc = [a + jnp.where(cells, e, 0.0) for a, e in zip(acc, terms)] + [
            acc[6] + jnp.where(pairs, fold(w * roll(w, 127, 1)), 0.0)
        ]
        first = first + jnp.where(jnp.logical_and(cells, plane8 == 2), ww, 0.0)
    first = jnp.where(ta == 0, first, 0.0)
    acc = acc[:5] + [2.0 * (acc[5] + acc[6]) + first]
    lane1 = lax.broadcasted_iota(jnp.int32, (1, 128), 1)
    row = jnp.zeros((1, 128), F32)
    for i, v in enumerate(acc):
        row = jnp.where(lane1 == i, jnp.sum(v, keepdims=True), row)

    def send_all(buf, row, peers, send, recv):
        n = len(peers)
        buf[0] = row
        for i, peer in enumerate(peers):
            pltpu.make_async_remote_copy(
                src_ref=buf.at[0], dst_ref=buf.at[i + 1], send_sem=send, recv_sem=recv,
                device_id=peer, device_id_type=MESH,
            ).start()
        return pltpu.make_async_remote_copy(
            src_ref=buf.at[1 : n + 1], dst_ref=buf.at[1 : n + 1], send_sem=send, recv_sem=recv,
            device_id=peers[0], device_id_type=MESH,
        )

    def sum_all(buf, n):
        total = buf[0]
        for i in range(n):
            total = total + buf[i + 1]
        return total

    sent_a = send_all(buf_a, row, peers_a, ra_send, ra_recv)

    def differences(i, e):
        sl, sr = strips[0][i], strips[1][i]

        def whole(p):
            v = jnp.where(lane72 < 3, roll(sl, 126 - 8 * p, 1), e[p])
            return jnp.where(lane72 >= 126, roll(sr, 123 - 8 * p, 1), v)

        def step(t, v):
            p = t + 2
            nxt = whole(p + 1)
            v64 = v[0:64]
            hi = roll(jnp.where(lane64 == 0, roll(sr[0:64], 123 - 8 * p, 1), v64), 127, 1)
            diffs[i, 0, t] = v64 - nxt[0:64]
            diffs[i, 1, t] = v64 - roll(v, XR - 1, 0)[0:64]
            diffs[i, 2, t] = v64 - hi
            return nxt

        lax.fori_loop(0, 8, step, whole(2))

    for i, e in enumerate((eb, e1, e2)):
        differences(i, e)

    sent_a.wait_recv()
    row = sum_all(buf_a, len(peers_a))
    sent_b = send_all(buf_b, row, peers_b, rb_send, rb_recv)
    sent_b.wait_recv()
    row = sum_all(buf_b, len(peers_b))
    n = [jnp.sum(jnp.where(lane1 == i, row, 0.0), axis=1, keepdims=True) for i in range(6)]

    g0, g1, g2, g3, g4 = (6.0 * n[i] - n[i + 1] for i in range(5))
    l1, l2 = g1 / g0, g2 / g0
    d1 = g2 - l1 * g1
    f1 = g3 - l2 * g1
    l3 = f1 / d1
    d2 = g4 - l2 * g2 - l3 * f1
    y1 = n[1] - l1 * n[0]
    y2 = n[2] - l2 * n[0] - l3 * y1
    c2 = y2 / d2
    c1 = y1 / d1 - l3 * c2
    c0 = n[0] / g0 - l1 * c1 - l2 * c2
    c0, c1, c2 = (jnp.broadcast_to(v, (64, 128)) for v in (c0, c1, c2))

    def finish(t, _):
        for k, (old, out) in enumerate(((mass, mo_ref), (px, xo_ref), (py, yo_ref))):
            step = c0 * diffs[0, k, t] + c1 * diffs[1, k, t] + c2 * diffs[2, k, t]
            out[t] = old[t] - step
        return 0

    lax.fori_loop(0, 8, finish, 0)
    sent_a.wait_send()
    sent_b.wait_send()


def store(a_ref, b_ref, c_ref, a_out, b_out, c_out, sem):
    pairs = ((a_ref, a_out), (b_ref, b_out), (c_ref, c_out))
    copies = [pltpu.make_async_copy(src, dst, sem.at[i]) for i, (src, dst) in enumerate(pairs)]
    for copy in copies:
        copy.start()
    for copy in copies:
        copy.wait()


def body(density, flux_x, flux_y, congestion, initial_density):
    block = jax.ShapeDtypeStruct((8, 64, 128), F32)
    vm = lambda *s: pltpu.VMEM(s, F32)
    dma = pltpu.SemaphoreType.DMA
    arrays = (density, flux_x, flux_y, congestion, initial_density)
    arrays = [pltpu.with_memory_space_constraint(a, pltpu.HBM) for a in arrays]
    outs = pl.pallas_call(
        kernel,
        out_shape=(block,) * 3,
        in_specs=[pl.BlockSpec(memory_space=pltpu.HBM)] * 5,
        out_specs=[pl.BlockSpec(memory_space=pltpu.VMEM)] * 3,
        scratch_shapes=[vm(8, 64, 128)] * 4
        + [vm(64, 128)]
        + [vm(8, 64, 128)] * 3
        + [vm(TP, XR, 128)] * 3
        + [vm(16, 128)] * 2
        + [vm(XR, 128)] * 5
        + [vm(3, 3, 8, 64, 128)]
        + [vm(32, 128)] * 2
        + [vm(16, 128)] * 4
        + [vm(32, 128)] * 2
        + [vm(16, 128)] * 4
        + [vm(XR, 128)] * 4
        + [vm(16, 1, 128), vm(32, 1, 128)]
        + [dma((5,)), dma((15,)), dma((15,))]
        + [dma] * 4,
        compiler_params=pltpu.CompilerParams(
            collective_id=0, has_side_effects=True, vmem_limit_bytes=VMEM_MAIN
        ),
        name="prox_project",
    )(*arrays)
    return pl.pallas_call(
        store,
        out_shape=(block,) * 3,
        in_specs=[pl.BlockSpec(memory_space=pltpu.VMEM)] * 3,
        out_specs=[pl.BlockSpec(memory_space=pltpu.HBM)] * 3,
        scratch_shapes=[dma((3,))],
        compiler_params=pltpu.CompilerParams(vmem_limit_bytes=VMEM_STORE),
        name="store",
    )(*outs)


def solution(mesh):
    spec = P("ta", "gx", "gy")
    return jax.shard_map(
        body,
        mesh=mesh,
        in_specs=(spec,) * 4 + (P("gx", "gy"),),
        out_specs=(spec,) * 3,
        check_vma=False,
    )
```

time: 47.4 us -> 39.4 us (0.83)
  Pallas kernels: 43.1 us -> 38.4 us
  local copies, waits for them, and re-layouts: 3.46 us -> 0 us
    pallas_call x1, Pallas kernels: 43.1 us -> 37.5 us  [body(): pl.pallas_call(kernel, out_shape=(block,) * 3, in_specs=[pl.BlockSpec(mem...]
    unnamed x7 -> x0, local copies, waits for them, and re-layouts: 3.46 us -> none
    pallas_call x0 -> x1, Pallas kernels: none -> 0.9 us  [body(): pl.pallas_call(store, out_shape=(block,) * 3, in_specs=[pl.BlockSpec(memo...]
where the time goes in v2:
time: 39.4 us; the launch traced here: 39.1 us
  Pallas kernels  38.4 us (97%)
  between operations  0.64 us (2%)
    pallas_call x1, Pallas kernels, body(): pl.pallas_call(kernel, out_shape=(block,) * 3, in_specs=[pl.BlockSpec(mem...  37.5 us
    pallas_call x1, Pallas kernels, body(): pl.pallas_call(store, out_shape=(block,) * 3, in_specs=[pl.BlockSpec(memo...  0.9 us

profile of v2, /device:TPU:1, one launch (start us, length us, event | category | flops | bytes accessed | tf_op | source)
XLA Modules:
  0.0 39.1 jit_solution(14441209195173975563)
XLA Ops:
  0.6 37.5 %prox_project.1 = (f32[8,64,128]{2,1,0:T(8,128)S(1)}, f32[8,64,128]{2,1,0:T(8,128)S(1)}, f32[8,64,128]{2,1,0:T(8,128)S(1)}) custom-call(f32[8,64,128]{2,1,0:T(8,128)} %d_hbm.1, f32[8,64,128]{2,1,0:T(8,128)} %fx_hbm.1, f32[8,64,128]{2,1,0:T(8,128)} %fy_hbm.1, f32[8,64,128]{2,1,0:T(8,128)} %c_hbm.1, f32[64,128]{1,0:T(8,128)} %i_hbm.1), custom_call_target="tpu_custom_call" | custom-call | tf_op jit(solution)/shard_map/prox_project/pallas_call | solution.py:456
  38.1 0.9 %store.1 = (f32[8,64,128]{2,1,0:T(8,128)}, f32[8,64,128]{2,1,0:T(8,128)}, f32[8,64,128]{2,1,0:T(8,128)}) custom-call(f32[8,64,128]{2,1,0:T(8,128)S(1)} %get-tuple-element.6.a_ref, f32[8,64,128]{2,1,0:T(8,128)S(1)} %get-tuple-element.7.b_ref, f32[8,64,128]{2,1,0:T(8,128)S(1)} %get-tuple-element.8.c_ref), custom_call_target="tpu_custom_call" | custom-call | tf_op jit(solution)/shard_map/store/pallas_call | solution.py:481

commit v3 on v2

--- a/solution.py
+++ b/solution.py
@@ -59,39 +59,6 @@
     def at(dt, gx):
         return (ta + dt, gx, c["gy"])
 
-    bar = pltpu.get_barrier_semaphore()
-
-    def greet(peer):
-        pl.semaphore_signal(bar, inc=1, device_id=peer, device_id_type=MESH)
-
-    for peer in peers_b:
-        greet(peer)
-
-    odd = lax.rem(ta, 2) == 1
-    away_p = jnp.logical_and(has_p, odd)
-    away_m = jnp.logical_and(has_m, jnp.logical_not(odd))
-
-    @pl.when(has_p)
-    def _():
-        greet(at(1, gxp))
-        greet(at(1, gxm))
-
-    @pl.when(has_m)
-    def _():
-        greet(at(-1, gxp))
-        greet(at(-1, gxm))
-
-    @pl.when(away_p)
-    def _():
-        greet(at(1, c["gx"]))
-
-    @pl.when(away_m)
-    def _():
-        greet(at(-1, c["gx"]))
-
-    for peer in peers_a:
-        greet(peer)
-
     loads = [
         pltpu.make_async_copy(a, b, in_sem.at[i])
         for i, (a, b) in enumerate(
@@ -100,6 +67,40 @@
     ]
     for copy in loads:
         copy.start()
+
+    bar = pltpu.get_barrier_semaphore()
+
+    def greet(peer):
+        pl.semaphore_signal(bar, inc=1, device_id=peer, device_id_type=MESH)
+
+    odd = lax.rem(ta, 2) == 1
+    away_p = jnp.logical_and(has_p, odd)
+    away_m = jnp.logical_and(has_m, jnp.logical_not(odd))
+
+    @pl.when(has_p)
+    def _():
+        greet(at(1, gxp))
+        greet(at(1, gxm))
+
+    @pl.when(has_m)
+    def _():
+        greet(at(-1, gxp))
+        greet(at(-1, gxm))
+
+    for peer in peers_b:
+        greet(peer)
+
+    @pl.when(away_p)
+    def _():
+        greet(at(1, c["gx"]))
+
+    @pl.when(away_m)
+    def _():
+        greet(at(-1, c["gx"]))
+
+    for peer in peers_a:
+        greet(peer)
+
     for copy in loads:
         copy.wait()
 
@@ -291,7 +292,9 @@
         return tuple(jnp.where(here, r, strip) for r, strip in zip(shifted, strips))
 
     zero8, zero72 = jnp.zeros((8, 128), F32), jnp.zeros((XR, 128), F32)
-    left, right = lax.fori_loop(0, TP, pack, (zero72, zero72))
+    left, right = zero72, zero72
+    for p in range(TP):
+        left, right = pack(p, (left, right))
     s_yp[...] = jnp.where(slot72 == 5, py0, right)
     s_ym[...] = left
     y_p = remote(13, s_yp, r_ym, (ta, c["gx"], gyp))

time: 39.4 us -> 38.6 us (0.980)
  Pallas kernels: 38.4 us -> 37.6 us
    pallas_call x1, Pallas kernels: 37.5 us -> 36.7 us  [body(): pl.pallas_call(kernel, out_shape=(block,) * 3, in_specs=[pl.BlockSpec(mem...]
where the time goes in v3:
time: 38.6 us; the launch traced here: 38.2 us
  Pallas kernels  37.6 us (97%)
  between operations  0.64 us (2%)
    pallas_call x1, Pallas kernels, body(): pl.pallas_call(kernel, out_shape=(block,) * 3, in_specs=[pl.BlockSpec(mem...  36.7 us
    pallas_call x1, Pallas kernels, body(): pl.pallas_call(store, out_shape=(block,) * 3, in_specs=[pl.BlockSpec(memo...  0.9 us

profile of v3, /device:TPU:1, one launch (start us, length us, event | category | flops | bytes accessed | tf_op | source)
XLA Modules:
  0.0 38.2 jit_solution(3923465311166962238)
XLA Ops:
  0.6 36.7 %prox_project.1 = (f32[8,64,128]{2,1,0:T(8,128)S(1)}, f32[8,64,128]{2,1,0:T(8,128)S(1)}, f32[8,64,128]{2,1,0:T(8,128)S(1)}) custom-call(f32[8,64,128]{2,1,0:T(8,128)} %d_hbm.1, f32[8,64,128]{2,1,0:T(8,128)} %fx_hbm.1, f32[8,64,128]{2,1,0:T(8,128)} %fy_hbm.1, f32[8,64,128]{2,1,0:T(8,128)} %c_hbm.1, f32[64,128]{1,0:T(8,128)} %i_hbm.1), custom_call_target="tpu_custom_call" | custom-call | tf_op jit(solution)/shard_map/prox_project/pallas_call | solution.py:459
  37.3 0.9 %store.1 = (f32[8,64,128]{2,1,0:T(8,128)}, f32[8,64,128]{2,1,0:T(8,128)}, f32[8,64,128]{2,1,0:T(8,128)}) custom-call(f32[8,64,128]{2,1,0:T(8,128)S(1)} %get-tuple-element.6.a_ref, f32[8,64,128]{2,1,0:T(8,128)S(1)} %get-tuple-element.7.b_ref, f32[8,64,128]{2,1,0:T(8,128)S(1)} %get-tuple-element.8.c_ref), custom_call_target="tpu_custom_call" | custom-call | tf_op jit(solution)/shard_map/store/pallas_call | solution.py:484

commit v4 on v3

--- a/solution.py
+++ b/solution.py
@@ -47,7 +47,7 @@
     s_xp, s_xm, s_pp, s_pm, s_mp, s_mm,
     r_xm, r_xp, r_mm, r_mp, r_pm, r_pp,
     s_yp, s_ym, r_ym, r_yp, buf_a, buf_b,
-    in_sem, ss, rs, ra_send, ra_recv, rb_send, rb_recv,
+    in_sem, ss, rs, ra_send, ra_recv, rb_send, rb_recv, met,
 ):
     c = {a: lax.axis_index(a) for a in ("ta", "gx", "gy")}
     ta = c["ta"]
@@ -73,9 +73,17 @@
     def greet(peer):
         pl.semaphore_signal(bar, inc=1, device_id=peer, device_id_type=MESH)
 
-    odd = lax.rem(ta, 2) == 1
+    core, x, y = lax.rem(ta, 2), lax.rem(c["gx"], 4), (c["gx"] // 4) * 4 + ta // 2
+    odd = core == 1
     away_p = jnp.logical_and(has_p, odd)
     away_m = jnp.logical_and(has_m, jnp.logical_not(odd))
+    mate = at(1 - 2 * core, c["gx"])
+    ring_x = [at(0, (c["gx"] // 4) * 4 + lax.rem(x + d, 4)) for d in (2, 1, 3)]
+    ring_z = [(ta, c["gx"], lax.rem(c["gy"] + d, 8)) for d in (4, 3, 5, 2, 6, 1, 7)]
+    ring_y = []
+    for d in (4, 3, 5, 2, 6, 1, 7):
+        yy = lax.rem(y + d, 8)
+        ring_y.append((lax.rem(yy, 4) * 2 + core, (yy // 4) * 4 + x, c["gy"]))
 
     @pl.when(has_p)
     def _():
@@ -87,7 +95,15 @@
         greet(at(-1, gxp))
         greet(at(-1, gxm))
 
-    for peer in peers_b:
+    @pl.when(x == 3)
+    def _():
+        greet(at(0, gxp))
+
+    @pl.when(x == 0)
+    def _():
+        greet(at(0, gxm))
+
+    for peer in ring_y + ring_z + ring_x:
         greet(peer)
 
     @pl.when(away_p)
@@ -98,8 +114,7 @@
     def _():
         greet(at(-1, c["gx"]))
 
-    for peer in peers_a:
-        greet(peer)
+    greet(mate)
 
     for copy in loads:
         copy.wait()
@@ -145,25 +160,27 @@
     s_xp[26:28, :] = pyo[62:64, :]
     s_xm[24:27, :] = m7[0:3]
     s_xm[27:30, :] = pyo[0:3, :]
-    for j in range(2):
-        s_pp[2 * j : 2 * j + 2, :] = eb[8 + j, 62:64, :]
-        s_pm[3 * j : 3 * j + 3, :] = eb[8 + j, 0:3, :]
-    s_pp[4:6, :] = px0[8:10, :]
-    s_pp[6:8, :] = m7[62:64]
-    s_pp[8:10, :] = pyo[62:64, :]
-    s_pm[6:9, :] = m7[0:3]
-    s_pm[9:12, :] = pyo[0:3, :]
-    for j in range(3):
-        s_mp[2 * j : 2 * j + 2, :] = eb[2 + j, 62:64, :]
-        s_mm[3 * j : 3 * j + 3, :] = eb[2 + j, 0:3, :]
-    s_mp[6:9, :] = px0[2:5, :]
-    s_mp[9:11, :] = pyo[62:64, :]
-    s_mm[9:12, :] = pyo[0:3, :]
+    s_pp[0:1, :] = eb[9, 63:64, :]
+    s_pp[1:3, :] = px0[8:10, :]
+    s_pp[3:5, :] = m7[62:64]
+    s_pp[5:6, :] = pyo[63:64, :]
+    s_pm[0:2, :] = eb[9, 0:2, :]
+    s_pm[2:3, :] = eb[8, 0:1, :]
+    s_pm[3:6, :] = m7[0:3]
+    s_pm[6:8, :] = pyo[0:2, :]
+    s_mp[0:2, :] = eb[2, 62:64, :]
+    s_mp[2:3, :] = eb[3, 63:64, :]
+    s_mp[3:6, :] = px0[2:5, :]
+    s_mp[6:8, :] = pyo[62:64, :]
+    s_mm[0:2, :] = eb[2, 0:2, :]
+    s_mm[2:3, :] = eb[3, 0:1, :]
+    s_mm[3:5, :] = pyo[0:2, :]
+
     def one(flag):
         return jnp.where(flag, 1, 0)
 
-    greeted = len(peers_a) + len(peers_b) + 2 * one(has_p) + 2 * one(has_m)
-    pl.semaphore_wait(bar, greeted + one(away_p) + one(away_m))
+    greeted = len(ring_x + ring_y + ring_z) + 1 + 2 * one(has_p) + 2 * one(has_m)
+    pl.semaphore_wait(bar, greeted + one(away_p) + one(away_m) + one(x == 3) + one(x == 0))
 
     def remote(i, src, dst, peer):
         return pltpu.make_async_remote_copy(
@@ -212,6 +229,9 @@
         for copy in t_p[2:]:
             copy.start()
 
+    for peer in ring_x + [mate]:
+        pl.semaphore_signal(met, inc=1, device_id=peer, device_id_type=MESH)
+
     m0[0:64, :] = m7
 
     x_p.wait()
@@ -240,26 +260,27 @@
     def _():
         for copy in t_p:
             copy.wait_recv()
-        for j in range(2):
-            eb[j, 64:67, :] = r_mp[3 * j : 3 * j + 3, :]
-            eb[j, 70:72, :] = r_mm[2 * j : 2 * j + 2, :]
-        pxm[0:2, :] = r_mm[4:6, :]
-        mm[64:67, :] = r_mp[6:9, :]
-        mm[70:72, :] = r_mm[6:8, :]
-        pyl[64:67, :] = r_mp[9:12, :]
-        pyl[70:72, :] = r_mm[8:10, :]
+        eb[1, 71:72, :] = r_mm[0:1, :]
+        pxm[0:2, :] = r_mm[1:3, :]
+        mm[70:72, :] = r_mm[3:5, :]
+        pyl[71:72, :] = r_mm[5:6, :]
+        eb[1, 64:66, :] = r_mp[0:2, :]
+        eb[0, 64:65, :] = r_mp[2:3, :]
+        mm[64:67, :] = r_mp[3:6, :]
+        pyl[64:66, :] = r_mp[6:8, :]
         eb[2] = eb[2] - mm[...]
 
     @pl.when(has_p)
     def _():
         for copy in t_m:
             copy.wait_recv()
-        for j in range(3):
-            eb[10 + j, 64:67, :] = r_pp[3 * j : 3 * j + 3, :]
-            eb[10 + j, 70:72, :] = r_pm[2 * j : 2 * j + 2, :]
-        pxm[10:13, :] = r_pm[6:9, :]
-        pyh[64:67, :] = r_pp[9:12, :]
-        pyh[70:72, :] = r_pm[9:11, :]
+        eb[10, 70:72, :] = r_pm[0:2, :]
+        eb[11, 71:72, :] = r_pm[2:3, :]
+        pxm[10:13, :] = r_pm[3:6, :]
+        pyh[70:72, :] = r_pm[6:8, :]
+        eb[10, 64:66, :] = r_pp[0:2, :]
+        eb[11, 64:65, :] = r_pp[2:3, :]
+        pyh[64:66, :] = r_pp[3:5, :]
         eb[10] = eb[10] - m0[...]
 
     for p in range(TP):
@@ -386,6 +407,7 @@
             total = total + buf[i + 1]
         return total
 
+    pl.semaphore_wait(met, len(ring_x) + 1)
     sent_a = send_all(buf_a, row, peers_a, ra_send, ra_recv)
 
     def differences(i, e):
@@ -469,13 +491,14 @@
         + [vm(XR, 128)] * 5
         + [vm(3, 3, 8, 64, 128)]
         + [vm(32, 128)] * 2
-        + [vm(16, 128)] * 4
+        + [vm(8, 128)] * 4
         + [vm(32, 128)] * 2
-        + [vm(16, 128)] * 4
+        + [vm(8, 128)] * 4
         + [vm(XR, 128)] * 4
         + [vm(16, 1, 128), vm(32, 1, 128)]
         + [dma((5,)), dma((15,)), dma((15,))]
-        + [dma] * 4,
+        + [dma] * 4
+        + [pltpu.SemaphoreType.REGULAR],
         compiler_params=pltpu.CompilerParams(
             collective_id=0, has_side_effects=True, vmem_limit_bytes=VMEM_MAIN
         ),

time: 38.6 us -> 38.1 us (0.987)
  Pallas kernels: 37.6 us -> 37.1 us
    pallas_call x1, Pallas kernels: 36.7 us -> 36.2 us  [body(): pl.pallas_call(kernel, out_shape=(block,) * 3, in_specs=[pl.BlockSpec(mem...]
where the time goes in v4:
time: 38.1 us; the launch traced here: 37.8 us
  Pallas kernels  37.1 us (97%)
  between operations  0.64 us (2%)
    pallas_call x1, Pallas kernels, body(): pl.pallas_call(kernel, out_shape=(block,) * 3, in_specs=[pl.BlockSpec(mem...  36.2 us
    pallas_call x1, Pallas kernels, body(): pl.pallas_call(store, out_shape=(block,) * 3, in_specs=[pl.BlockSpec(memo...  0.9 us

profile of v4, /device:TPU:1, one launch (start us, length us, event | category | flops | bytes accessed | tf_op | source)
XLA Modules:
  0.0 37.8 jit_solution(10706709275152324646)
XLA Ops:
  0.6 36.2 %prox_project.1 = (f32[8,64,128]{2,1,0:T(8,128)S(1)}, f32[8,64,128]{2,1,0:T(8,128)S(1)}, f32[8,64,128]{2,1,0:T(8,128)S(1)}) custom-call(f32[8,64,128]{2,1,0:T(8,128)} %d_hbm.1, f32[8,64,128]{2,1,0:T(8,128)} %fx_hbm.1, f32[8,64,128]{2,1,0:T(8,128)} %fy_hbm.1, f32[8,64,128]{2,1,0:T(8,128)} %c_hbm.1, f32[64,128]{1,0:T(8,128)} %i_hbm.1), custom_call_target="tpu_custom_call" | custom-call | tf_op jit(solution)/shard_map/prox_project/pallas_call | solution.py:481
  36.9 0.9 %store.1 = (f32[8,64,128]{2,1,0:T(8,128)}, f32[8,64,128]{2,1,0:T(8,128)}, f32[8,64,128]{2,1,0:T(8,128)}) custom-call(f32[8,64,128]{2,1,0:T(8,128)S(1)} %get-tuple-element.6.a_ref, f32[8,64,128]{2,1,0:T(8,128)S(1)} %get-tuple-element.7.b_ref, f32[8,64,128]{2,1,0:T(8,128)S(1)} %get-tuple-element.8.c_ref), custom_call_target="tpu_custom_call" | custom-call | tf_op jit(solution)/shard_map/store/pallas_call | solution.py:507

commit v5 on v4

--- a/solution.py
+++ b/solution.py
@@ -12,6 +12,7 @@
 NEWTON = 6
 F32 = jnp.float32
 TP, XR = 13, 72
+SHIFT, SHIFTS = 4.0, 4
 VMEM_MAIN, VMEM_STORE = 16 * 2**20, 2**20
 
 
@@ -59,15 +60,6 @@
     def at(dt, gx):
         return (ta + dt, gx, c["gy"])
 
-    loads = [
-        pltpu.make_async_copy(a, b, in_sem.at[i])
-        for i, (a, b) in enumerate(
-            ((d_hbm, d_ref), (fx_hbm, fx_ref), (fy_hbm, fy_ref), (c_hbm, c_ref), (i_hbm, i_ref))
-        )
-    ]
-    for copy in loads:
-        copy.start()
-
     bar = pltpu.get_barrier_semaphore()
 
     def greet(peer):
@@ -102,6 +94,15 @@
     @pl.when(x == 0)
     def _():
         greet(at(0, gxm))
+
+    loads = [
+        pltpu.make_async_copy(a, b, in_sem.at[i])
+        for i, (a, b) in enumerate(
+            ((d_hbm, d_ref), (fx_hbm, fx_ref), (fy_hbm, fy_ref), (c_hbm, c_ref), (i_hbm, i_ref))
+        )
+    ]
+    for copy in loads:
+        copy.start()
 
     for peer in ring_y + ring_z + ring_x:
         greet(peer)
@@ -316,8 +317,13 @@
     left, right = zero72, zero72
     for p in range(TP):
         left, right = pack(p, (left, right))
-    s_yp[...] = jnp.where(slot72 == 5, py0, right)
-    s_ym[...] = left
+    half = lax.rem(lax.broadcasted_iota(jnp.int32, (32, 128), 1), 8) < 4
+    v = roll(jnp.where(slot72 == 5, py0, right), 125, 1)
+    s_yp[0:32, :] = jnp.where(half, v[0:32], roll(v[40:72], 4, 1))
+    s_yp[32:40, :] = v[32:40]
+    v = roll(left, 3, 1)
+    s_ym[0:32, :] = jnp.where(half, roll(v[40:72], 124, 1), v[0:32])
+    s_ym[32:40, :] = v[32:40]
     y_p = remote(13, s_yp, r_ym, (ta, c["gx"], gyp))
     y_m = remote(14, s_ym, r_yp, (ta, c["gx"], gym))
     y_p.start()
@@ -327,7 +333,8 @@
         def step(p, _):
             v = src[p]
             ends = roll(v, 1, 1) + roll(v, 127, 1)
-            dst[p] = (src[p - 1] + src[p + 1]) + (roll(v, 1, 0) + roll(v, XR - 1, 0)) + ends
+            near = (src[p - 1] + src[p + 1]) + (roll(v, 1, 0) + roll(v, XR - 1, 0)) + ends
+            dst[p] = 6.0 * v - near
             return 0
 
         return step
@@ -335,58 +342,79 @@
     def fold(v):
         return jnp.sum(v.reshape(8, 8, 128), axis=0)
 
+    def shifted(b, u, w, k):
+        v = u - k * SHIFT * b
+        return v, (w - k * SHIFT * u) - k * SHIFT * v
+
+    def edges(w, later):
+        dx, dy = w - roll(w, XR - 1, 0), w - roll(w, 127, 1)
+        dt, dx, dy = w[0:64] - later, dx[0:64], dy[0:64]
+        return fold(dt * dt + dx * dx), fold(dy * dy)
+
     def moments(p, acc):
-        b, u, full = eb[p, 0:64, :], e1[p, 0:64, :], e2[p]
-        w = full[0:64]
-        later = e2[p + 1, 0:64, :] + roll(full, XR - 1, 0)[0:64]
-        terms = (b * b, b * u, u * u, u * w, w * w, w * later, w * roll(w, 127, 1))
-        return tuple(a + fold(v) for a, v in zip(acc, terms))
-
-    lax.fori_loop(1, 12, spread(eb, e1), 0)
-    lax.fori_loop(2, 11, spread(e1, e2), 0)
-    acc = lax.fori_loop(2, 10, moments, (zero8,) * 7)
-    w0 = e2[2, 0:64, :]
-    first = fold(w0 * w0)
+        here, nxt = (eb[p], e1[p], e2[p]), (eb[p + 1, 0:64, :], e1[p + 1, 0:64, :], e2[p + 1, 0:64, :])
+        b = here[0][0:64]
+        terms = [fold(b * b)]
+        for k in range(SHIFTS):
+            v, w = shifted(*here, k)
+            e = edges(w, shifted(*nxt, k)[1])
+            v, w = v[0:64], w[0:64]
+            terms += [fold(b * v), fold(v * v), fold(v * w), fold(w * w), *e]
+        return tuple(a + t for a, t in zip(acc, terms))
+
+    for p in range(1, 12):
+        spread(eb, e1)(p, 0)
+    for p in range(2, 11):
+        spread(e1, e2)(p, 0)
+    acc = lax.fori_loop(2, 10, moments, (zero8,) * (1 + 6 * SHIFTS))
 
     y_p.wait()
     y_m.wait()
-    near = roll(r_ym[...], 125, 1)
+    v = r_ym[...]
+    near = jnp.concatenate([v, roll(v[0:32], 124, 1)], 0)
     left = jnp.where(slot72 < 2, near, left) - jnp.where(slot72 == 2, near, 0.0)
-    near = roll(r_yp[...], 3, 1)
+    v = r_yp[...]
+    near = jnp.concatenate([v, roll(v[0:32], 4, 1)], 0)
     right = jnp.where(slot72 >= 5, near, right) - jnp.where(slot72 == 5, py0, 0.0)
 
-    def around(v):
-        return (
+    def apply(v):
+        return 6.0 * v - (
             (roll(v, 8, 1) + roll(v, 120, 1))
             + (roll(v, 1, 0) + roll(v, XR - 1, 0))
             + (roll(v, 1, 1) + roll(v, 127, 1))
         )
 
+    inner = jnp.logical_and(lane8 >= 3, lane8 < 126)
+    inner_y = jnp.logical_and(lane8 >= 3, lane8 < 125)
+    masks = [inner] + ([inner] * 5 + [inner_y]) * SHIFTS
+    acc = [jnp.where(mask, v, 0.0) for mask, v in zip(masks, acc)]
+    block = jnp.logical_and(plane8 >= 2, plane8 < 10)
+    pairs = jnp.logical_and(block, jnp.logical_and(slot8 >= 2, slot8 < 5))
     strips = []
-    inner = jnp.logical_and(lane8 >= 3, lane8 < 126)
-    acc = [jnp.where(inner, v, 0.0) for v in acc[:6]] + [jnp.where(lane8 == 125, 0.0, jnp.where(inner, acc[6], 0.0))]
-    first = jnp.where(inner, first, 0.0)
-    block = jnp.logical_and(plane8 >= 2, plane8 < 10)
-    for v, lo, hi in ((left, 2, 5), (right, 3, 5)):
-        u = around(v)
-        w = around(u)
-        strips.append((v, u, w))
-        later = (roll(w, 120, 1) + roll(w, XR - 1, 0))[0:64]
-        v, u, w = v[0:64], u[0:64], w[0:64]
-        cells = jnp.logical_and(block, jnp.logical_and(slot8 >= lo, slot8 < hi))
-        pairs = jnp.logical_and(block, jnp.logical_and(slot8 >= 2, slot8 < 5))
-        ww = fold(w * w)
-        terms = [fold(e) for e in (v * v, v * u, u * u, u * w)] + [ww, fold(w * later)]
-        acc = [a + jnp.where(cells, e, 0.0) for a, e in zip(acc, terms)] + [
-            acc[6] + jnp.where(pairs, fold(w * roll(w, 127, 1)), 0.0)
-        ]
-        first = first + jnp.where(jnp.logical_and(cells, plane8 == 2), ww, 0.0)
-    first = jnp.where(ta == 0, first, 0.0)
-    acc = acc[:5] + [2.0 * (acc[5] + acc[6]) + first]
-    lane1 = lax.broadcasted_iota(jnp.int32, (1, 128), 1)
-    row = jnp.zeros((1, 128), F32)
-    for i, v in enumerate(acc):
-        row = jnp.where(lane1 == i, jnp.sum(v, keepdims=True), row)
+    for b, lo in ((left, 2), (right, 3)):
+        u = apply(b)
+        strips.append((b, u, apply(u)))
+        cells = jnp.logical_and(block, jnp.logical_and(slot8 >= lo, slot8 < 5))
+        b64 = b[0:64]
+        terms = [fold(b64 * b64)]
+        for k in range(SHIFTS):
+            v, w = shifted(*strips[-1], k)
+            e = edges(w, roll(w, 120, 1)[0:64])
+            v, w = v[0:64], w[0:64]
+            terms += [fold(b64 * v), fold(v * v), fold(v * w), fold(w * w), *e]
+        masks = [cells] + ([cells] * 5 + [pairs]) * SHIFTS
+        acc = [a + jnp.where(mask, e, 0.0) for a, mask, e in zip(acc, masks, terms)]
+    sub8 = lax.broadcasted_iota(jnp.int32, (8, 128), 0)
+    spot = zero8
+    for j in range(6):
+        rows = zero8
+        for k in range(SHIFTS):
+            v = acc[0] if j == 0 else acc[6 * k + j]
+            if j == 5:
+                v = v + acc[6 * k + 6]
+            rows = jnp.where(sub8 == k, jnp.sum(v, axis=0, keepdims=True), rows)
+        spot = jnp.where(lane8 == 8 * j + sub8, jnp.sum(rows, axis=1, keepdims=True), spot)
+    row = jnp.sum(spot, axis=0, keepdims=True)
 
     def send_all(buf, row, peers, send, recv):
         n = len(peers)
@@ -437,20 +465,29 @@
     sent_b = send_all(buf_b, row, peers_b, rb_send, rb_recv)
     sent_b.wait_recv()
     row = sum_all(buf_b, len(peers_b))
-    n = [jnp.sum(jnp.where(lane1 == i, row, 0.0), axis=1, keepdims=True) for i in range(6)]
-
-    g0, g1, g2, g3, g4 = (6.0 * n[i] - n[i + 1] for i in range(5))
+    row = jnp.broadcast_to(row, (8, 128))
+    m0, m1, m2, m3, m4, g4 = (row if j == 0 else roll(row, 128 - 8 * j, 1) for j in range(6))
+    shift = SHIFT * lane8.astype(F32)
+    g0, g1, g2, g3 = shift * m0 + m1, shift * m1 + m2, shift * m2 + m3, shift * m3 + m4
     l1, l2 = g1 / g0, g2 / g0
     d1 = g2 - l1 * g1
     f1 = g3 - l2 * g1
-    l3 = f1 / d1
+    i1 = jnp.where(d1 > 0.0, 1.0 / d1, 0.0)
+    l3 = f1 * i1
     d2 = g4 - l2 * g2 - l3 * f1
-    y1 = n[1] - l1 * n[0]
-    y2 = n[2] - l2 * n[0] - l3 * y1
-    c2 = y2 / d2
-    c1 = y1 / d1 - l3 * c2
-    c0 = n[0] / g0 - l1 * c1 - l2 * c2
-    c0, c1, c2 = (jnp.broadcast_to(v, (64, 128)) for v in (c0, c1, c2))
+    y1 = m1 - l1 * m0
+    y2 = m2 - l2 * m0 - l3 * y1
+    c2 = jnp.where(d2 > 0.0, y2 / d2, 0.0)
+    c1 = y1 * i1 - l3 * c2
+    c0 = m0 / g0 - l1 * c1 - l2 * c2
+    c0, c1 = c0 - shift * (c1 - shift * c2), c1 - 2.0 * shift * c2
+    far = jnp.where(lane8 < SHIFTS, jnp.abs(m1), jnp.inf)
+    best = far == jnp.min(far, axis=1, keepdims=True)
+    count = jnp.sum(jnp.where(best, 1.0, 0.0), axis=1, keepdims=True)
+    c0, c1, c2 = (
+        jnp.sum(jnp.where(best, v, 0.0), axis=1, keepdims=True) / count for v in (c0, c1, c2)
+    )
+    c0, c1, c2 = (jnp.broadcast_to(v[0:1], (64, 128)) for v in (c0, c1, c2))
 
     def finish(t, _):
         for k, (old, out) in enumerate(((mass, mo_ref), (px, xo_ref), (py, yo_ref))):
@@ -494,7 +531,7 @@
         + [vm(8, 128)] * 4
         + [vm(32, 128)] * 2
         + [vm(8, 128)] * 4
-        + [vm(XR, 128)] * 4
+        + [vm(40, 128)] * 4
         + [vm(16, 1, 128), vm(32, 1, 128)]
         + [dma((5,)), dma((15,)), dma((15,))]
         + [dma] * 4

time: 38.1 us -> 38.3 us (level)
  no operation moved by 1% of the time
where the time goes in v5:
time: 38.3 us; the launch traced here: 38 us
  Pallas kernels  37.4 us (98%)
  between operations  0.64 us (2%)
    pallas_call x1, Pallas kernels, body(): pl.pallas_call(kernel, out_shape=(block,) * 3, in_specs=[pl.BlockSpec(mem...  36.5 us
    pallas_call x1, Pallas kernels, body(): pl.pallas_call(store, out_shape=(block,) * 3, in_specs=[pl.BlockSpec(memo...  0.9 us

profile of v5, /device:TPU:1, one launch (start us, length us, event | category | flops | bytes accessed | tf_op | source)
XLA Modules:
  0.0 38.0 jit_solution(7962864140688964584)
XLA Ops:
  0.6 36.5 %prox_project.1 = (f32[8,64,128]{2,1,0:T(8,128)S(1)}, f32[8,64,128]{2,1,0:T(8,128)S(1)}, f32[8,64,128]{2,1,0:T(8,128)S(1)}) custom-call(f32[8,64,128]{2,1,0:T(8,128)} %d_hbm.1, f32[8,64,128]{2,1,0:T(8,128)} %fx_hbm.1, f32[8,64,128]{2,1,0:T(8,128)} %fy_hbm.1, f32[8,64,128]{2,1,0:T(8,128)} %c_hbm.1, f32[64,128]{1,0:T(8,128)} %i_hbm.1), custom_call_target="tpu_custom_call" | custom-call | tf_op jit(solution)/shard_map/prox_project/pallas_call | solution.py:518
  37.1 0.9 %store.1 = (f32[8,64,128]{2,1,0:T(8,128)}, f32[8,64,128]{2,1,0:T(8,128)}, f32[8,64,128]{2,1,0:T(8,128)}) custom-call(f32[8,64,128]{2,1,0:T(8,128)S(1)} %get-tuple-element.6.a_ref, f32[8,64,128]{2,1,0:T(8,128)S(1)} %get-tuple-element.7.b_ref, f32[8,64,128]{2,1,0:T(8,128)S(1)} %get-tuple-element.8.c_ref), custom_call_target="tpu_custom_call" | custom-call | tf_op jit(solution)/shard_map/store/pallas_call | solution.py:544

commit v6 on v5

--- a/solution.py
+++ b/solution.py
@@ -13,7 +13,7 @@
 F32 = jnp.float32
 TP, XR = 13, 72
 SHIFT, SHIFTS = 4.0, 4
-VMEM_MAIN, VMEM_STORE = 16 * 2**20, 2**20
+VMEM_MAIN, VMEM_STORE = 16 * 2**20, 4 * 2**20
 
 
 def roll(v, shift, axis):
@@ -42,9 +42,9 @@
 
 def kernel(
     d_hbm, fx_hbm, fy_hbm, c_hbm, i_hbm,
-    mo_ref, xo_ref, yo_ref,
-    d_ref, fx_ref, fy_ref, c_ref, i_ref, mass, px, py,
-    eb, e1, e2, px0, pxm, m0, mm, pyo, pyl, pyh, diffs,
+    mass, px, py, diffs, coef,
+    d_ref, fx_ref, fy_ref, c_ref, i_ref,
+    eb, e1, e2, px0, pxm, m0, mm, pyo, pyl, pyh,
     s_xp, s_xm, s_pp, s_pm, s_mp, s_mm,
     r_xm, r_xp, r_mm, r_mp, r_pm, r_pp,
     s_yp, s_ym, r_ym, r_yp, buf_a, buf_b,
@@ -487,24 +487,27 @@
     c0, c1, c2 = (
         jnp.sum(jnp.where(best, v, 0.0), axis=1, keepdims=True) / count for v in (c0, c1, c2)
     )
-    c0, c1, c2 = (jnp.broadcast_to(v[0:1], (64, 128)) for v in (c0, c1, c2))
-
-    def finish(t, _):
-        for k, (old, out) in enumerate(((mass, mo_ref), (px, xo_ref), (py, yo_ref))):
-            step = c0 * diffs[0, k, t] + c1 * diffs[1, k, t] + c2 * diffs[2, k, t]
-            out[t] = old[t] - step
-        return 0
-
-    lax.fori_loop(0, 8, finish, 0)
+    for i, v in enumerate((c0, c1, c2)):
+        coef[i] = jnp.broadcast_to(v, (8, 128))
     sent_a.wait_send()
     sent_b.wait_send()
 
 
-def store(a_ref, b_ref, c_ref, a_out, b_out, c_out, sem):
-    pairs = ((a_ref, a_out), (b_ref, b_out), (c_ref, c_out))
-    copies = [pltpu.make_async_copy(src, dst, sem.at[i]) for i, (src, dst) in enumerate(pairs)]
-    for copy in copies:
-        copy.start()
+def store(m_ref, x_ref, y_ref, diffs, coef, m_out, x_out, y_out, m_buf, x_buf, y_buf, sem):
+    c0, c1, c2 = (jnp.concatenate([coef[i]] * 8, 0) for i in range(3))
+    copies = []
+    for k, (old, buf, out) in enumerate(
+        ((m_ref, m_buf, m_out), (x_ref, x_buf, x_out), (y_ref, y_buf, y_out))
+    ):
+
+        def plane(t, _, k=k, old=old, buf=buf):
+            step = c0 * diffs[0, k, t] + c1 * diffs[1, k, t] + c2 * diffs[2, k, t]
+            buf[t] = old[t] - step
+            return 0
+
+        lax.fori_loop(0, 8, plane, 0)
+        copies.append(pltpu.make_async_copy(buf, out, sem.at[k]))
+        copies[k].start()
     for copy in copies:
         copy.wait()
 
@@ -517,16 +520,16 @@
     arrays = [pltpu.with_memory_space_constraint(a, pltpu.HBM) for a in arrays]
     outs = pl.pallas_call(
         kernel,
-        out_shape=(block,) * 3,
+        out_shape=(block,) * 3 + tuple(
+            jax.ShapeDtypeStruct(shape, F32) for shape in ((3, 3, 8, 64, 128), (3, 8, 128))
+        ),
         in_specs=[pl.BlockSpec(memory_space=pltpu.HBM)] * 5,
-        out_specs=[pl.BlockSpec(memory_space=pltpu.VMEM)] * 3,
+        out_specs=[pl.BlockSpec(memory_space=pltpu.VMEM)] * 5,
         scratch_shapes=[vm(8, 64, 128)] * 4
         + [vm(64, 128)]
-        + [vm(8, 64, 128)] * 3
         + [vm(TP, XR, 128)] * 3
         + [vm(16, 128)] * 2
         + [vm(XR, 128)] * 5
-        + [vm(3, 3, 8, 64, 128)]
         + [vm(32, 128)] * 2
         + [vm(8, 128)] * 4
         + [vm(32, 128)] * 2
@@ -544,9 +547,9 @@
     return pl.pallas_call(
         store,
         out_shape=(block,) * 3,
-        in_specs=[pl.BlockSpec(memory_space=pltpu.VMEM)] * 3,
+        in_specs=[pl.BlockSpec(memory_space=pltpu.VMEM)] * 5,
         out_specs=[pl.BlockSpec(memory_space=pltpu.HBM)] * 3,
-        scratch_shapes=[dma((3,))],
+        scratch_shapes=[vm(8, 64, 128)] * 3 + [dma((3,))],
         compiler_params=pltpu.CompilerParams(vmem_limit_bytes=VMEM_STORE),
         name="store",
     )(*outs)

time: 38.3 us -> 38.3 us (level)
  no operation moved by 1% of the time
where the time goes in v6:
time: 38.3 us; the launch traced here: 38 us
  Pallas kernels  37.3 us (97%)
  between operations  0.64 us (2%)
    pallas_call x1, Pallas kernels, body(): pl.pallas_call(kernel, out_shape=(block,) * 3 + tuple((jax.ShapeDtypeStru...  36.3 us
    pallas_call x1, Pallas kernels, body(): pl.pallas_call(store, out_shape=(block,) * 3, in_specs=[pl.BlockSpec(memo...  1.04 us

profile of v6, /device:TPU:1, one launch (start us, length us, event | category | flops | bytes accessed | tf_op | source)
XLA Modules:
  0.0 38.0 jit_solution(6857142932669890308)
XLA Ops:
  0.6 36.3 %prox_project.1 = (f32[8,64,128]{2,1,0:T(8,128)S(1)}, f32[8,64,128]{2,1,0:T(8,128)S(1)}, f32[8,64,128]{2,1,0:T(8,128)S(1)}, f32[3,3,8,64,128]{4,3,2,1,0:T(8,128)S(1)}, f32[3,8,128]{2,1,0:T(8,128)S(1)}) custom-call(f32[8,64,128]{2,1,0:T(8,128)} %d_hbm.1, f32[8,64,128]{2,1,0:T(8,128)} %fx_hbm.1, f32[8,64,128]{2,1,0:T(8,128)} %fy_hbm.1, f32[8,64,128]{2,1,0:T(8,128)} %c_hbm.1, ...), custom_call_target="tpu_custom_call" | custom-call | tf_op jit(solution)/shard_map/prox_project/pallas_call | solution.py:521
  36.9 1.0 %store.1 = (f32[8,64,128]{2,1,0:T(8,128)}, f32[8,64,128]{2,1,0:T(8,128)}, f32[8,64,128]{2,1,0:T(8,128)}) custom-call(f32[8,64,128]{2,1,0:T(8,128)S(1)} %get-tuple-element.8.m_ref, f32[8,64,128]{2,1,0:T(8,128)S(1)} %get-tuple-element.9.x_ref, f32[8,64,128]{2,1,0:T(8,128)S(1)} %get-tuple-element.10.y_ref, f32[3,3,8,64,128]{4,3,2,1,0:T(8,128)S(1)} %get-tuple-element.11.diffs, ...), custom_call_target="tpu_custom_call" | custom-call | tf_op jit(solution)/shard_map/store/pallas_call | solution.py:547

commit v7 on v6

--- a/solution.py
+++ b/solution.py
@@ -505,9 +505,11 @@
             buf[t] = old[t] - step
             return 0
 
-        lax.fori_loop(0, 8, plane, 0)
-        copies.append(pltpu.make_async_copy(buf, out, sem.at[k]))
-        copies[k].start()
+        for h in (0, 4):
+            lax.fori_loop(h, h + 4, plane, 0)
+            copy = pltpu.make_async_copy(buf.at[h : h + 4], out.at[h : h + 4], sem.at[k, h // 4])
+            copy.start()
+            copies.append(copy)
     for copy in copies:
         copy.wait()
 
@@ -549,7 +551,7 @@
         out_shape=(block,) * 3,
         in_specs=[pl.BlockSpec(memory_space=pltpu.VMEM)] * 5,
         out_specs=[pl.BlockSpec(memory_space=pltpu.HBM)] * 3,
-        scratch_shapes=[vm(8, 64, 128)] * 3 + [dma((3,))],
+        scratch_shapes=[vm(8, 64, 128)] * 3 + [dma((3, 2))],
         compiler_params=pltpu.CompilerParams(vmem_limit_bytes=VMEM_STORE),
         name="store",
     )(*outs)

time: 38.3 us -> 38.2 us (level)
  no operation moved by 1% of the time
where the time goes in v7:
time: 38.2 us; the launch traced here: 37.9 us
  Pallas kernels  37.3 us (98%)
  between operations  0.64 us (2%)
    pallas_call x1, Pallas kernels, body(): pl.pallas_call(kernel, out_shape=(block,) * 3 + tuple((jax.ShapeDtypeStru...  36.3 us
    pallas_call x1, Pallas kernels, body(): pl.pallas_call(store, out_shape=(block,) * 3, in_specs=[pl.BlockSpec(memo...  1.02 us

profile of v7, /device:TPU:1, one launch (start us, length us, event | category | flops | bytes accessed | tf_op | source)
XLA Modules:
  0.0 37.9 jit_solution(9286880274297914110)
XLA Ops:
  0.6 36.3 %prox_project.1 = (f32[8,64,128]{2,1,0:T(8,128)S(1)}, f32[8,64,128]{2,1,0:T(8,128)S(1)}, f32[8,64,128]{2,1,0:T(8,128)S(1)}, f32[3,3,8,64,128]{4,3,2,1,0:T(8,128)S(1)}, f32[3,8,128]{2,1,0:T(8,128)S(1)}) custom-call(f32[8,64,128]{2,1,0:T(8,128)} %d_hbm.1, f32[8,64,128]{2,1,0:T(8,128)} %fx_hbm.1, f32[8,64,128]{2,1,0:T(8,128)} %fy_hbm.1, f32[8,64,128]{2,1,0:T(8,128)} %c_hbm.1, ...), custom_call_target="tpu_custom_call" | custom-call | tf_op jit(solution)/shard_map/prox_project/pallas_call | solution.py:523
  36.9 1.0 %store.1 = (f32[8,64,128]{2,1,0:T(8,128)}, f32[8,64,128]{2,1,0:T(8,128)}, f32[8,64,128]{2,1,0:T(8,128)}) custom-call(f32[8,64,128]{2,1,0:T(8,128)S(1)} %get-tuple-element.8.m_ref, f32[8,64,128]{2,1,0:T(8,128)S(1)} %get-tuple-element.9.x_ref, f32[8,64,128]{2,1,0:T(8,128)S(1)} %get-tuple-element.10.y_ref, f32[3,3,8,64,128]{4,3,2,1,0:T(8,128)S(1)} %get-tuple-element.11.diffs, ...), custom_call_target="tpu_custom_call" | custom-call | tf_op jit(solution)/shard_map/store/pallas_call | solution.py:549
